TPU v7x, 256 devices: a whole 4x4x8 slice. The times are simulated.
256 devices in a mesh: tm: 32 (over y, x, core), rows: 8 (over z).
Axes of the slice: x: 4, y: 4, z: 8, core: 2. Of those that a mesh axis runs over, the one named last changes fastest.
Arguments:
- tokens: bfloat16 [32, 64, 64, 768], P('tm', 'rows'), may hold values from -6 to 6
- col_shift: int32 [32], P('tm'), may hold values from 0 to 7
- frame_group: int32 [32], replicated, may hold values from 0 to 15, never falling along the last dimension, each value on 1 to 4 neighbouring positions
- spatial_qkv: bfloat16 [768, 2304], replicated
- spatial_out: bfloat16 [768, 768], replicated
- temporal_qkv: bfloat16 [768, 2304], replicated
- temporal_out: bfloat16 [768, 768], replicated, may hold values from -0.21875 to 0.21875
Outputs:
- layer_out: bfloat16 [32, 64, 64, 768], P('tm', 'rows')
Inputs may be any that keep to these rules, and one draw needn't show every extreme that they name: `frame_group`: never falls from one frame to the next and every group from 0 on appears.
All inputs are finite; a program needn't handle non-finite values.
Results may differ from a plain program's by a relative error of at most 0.008.
The roundings to bfloat16 on the way count: a program that leaves them out, or rounds other values in their place, can miss the bound.
Values may be sent and summed in bfloat16 or wider, within the bound.
A program may use at most 64 MiB of HBM per device.

v0:
```python
import math

import jax
import jax.numpy as jnp
from jax import lax
from jax.sharding import PartitionSpec as P

HEADS = 12
WIN = 8


def with_halo(block, sides, width):
    for axis, dim in sides:
        count = lax.axis_size(axis)
        forward = [(i, i + 1) for i in range(count - 1)]
        forward.append((count - 1, 0))
        backward = [(target, source) for source, target in forward]
        low = lax.ppermute(
            lax.slice_in_dim(block, block.shape[dim] - width, None, axis=dim), axis, forward
        )
        high = lax.ppermute(lax.slice_in_dim(block, 0, width, axis=dim), axis, backward)
        block = jnp.concatenate([low, block, high], axis=dim)
    return block


def normalize(values):
    widened = values.astype(jnp.float32)
    center = widened - jnp.mean(widened, axis=-1, keepdims=True)
    spread = jnp.mean(center * center, axis=-1, keepdims=True)
    return (center * lax.rsqrt(spread + 1e-05)).astype(jnp.bfloat16)


def project(values, weight):
    flattened = values.reshape(-1, values.shape[-1])
    product = jnp.dot(flattened, weight, preferred_element_type=jnp.float32)
    return product.reshape(values.shape[:-1] + (weight.shape[1],))


def split_heads(values):
    return values.reshape(values.shape[:-1] + (HEADS, values.shape[-1] // HEADS))


def attend(queries, key_rows, value_rows, allowed, score_form, mix_form):
    scale = 1.0 / math.sqrt(queries.shape[-1])
    scores = jnp.einsum(score_form, queries, key_rows, preferred_element_type=jnp.float32) * scale
    if allowed is not None:
        scores = jnp.where(allowed, scores, -1e30)
    maxima = jnp.max(scores, axis=-1, keepdims=True)
    raised = jnp.exp(scores - maxima)
    totals = jnp.sum(raised, axis=-1, keepdims=True)
    weights = (raised / totals).astype(jnp.bfloat16)
    mixed_rows = jnp.einsum(mix_form, weights, value_rows, preferred_element_type=jnp.float32)
    return mixed_rows.astype(jnp.bfloat16)


def roll_columns(values, offsets, direction):

    def one_frame(single_frame, offset):
        return jnp.roll(single_frame, direction * offset, axis=1)

    return jax.vmap(one_frame)(values, offsets)


def per_device(
    tokens, col_shift, frame_group, spatial_qkv, spatial_out, temporal_qkv, temporal_out
):
    frames_here, band_rows, columns, model_width = tokens.shape
    half_window = WIN // 2
    time_count = lax.axis_size("tm")
    normed = normalize(tokens)
    queries = project(normed, spatial_qkv[:, :model_width]).astype(jnp.bfloat16)
    own_pairs = project(normed, spatial_qkv[:, model_width:]).astype(jnp.bfloat16)
    key_value = with_halo(own_pairs, (("rows", 1),), half_window)
    padding = jnp.zeros((frames_here, half_window) + queries.shape[2:], jnp.bfloat16)
    query_rows = jnp.concatenate([padding, queries, padding], axis=1)
    query_rows = roll_columns(query_rows, col_shift, -1)
    key_value = roll_columns(key_value, col_shift, -1)
    window_rows = (band_rows + WIN) // WIN
    window_cols = columns // WIN

    def to_windows(values):
        width = values.shape[-1]
        shaped = values.reshape(frames_here, window_rows, WIN, window_cols, WIN, width)
        return shaped.transpose(0, 1, 3, 2, 4, 5).reshape(-1, WIN * WIN, width)

    query_windows = to_windows(query_rows)
    pair_windows = to_windows(key_value)
    attended = attend(
        split_heads(query_windows),
        split_heads(pair_windows[:, :, :model_width]),
        split_heads(pair_windows[:, :, model_width:]),
        None,
        "bnhd,bmhd->bhnm",
        "bhnm,bmhd->bnhd",
    )
    attended = attended.reshape(frames_here, window_rows, window_cols, WIN, WIN, model_width)
    attended = attended.transpose(0, 1, 3, 2, 4, 5).reshape(
        frames_here, band_rows + WIN, columns, model_width
    )
    attended = roll_columns(attended, col_shift, 1)[:, half_window : half_window + band_rows]
    stream = (tokens.astype(jnp.float32) + project(attended, spatial_out)).astype(jnp.bfloat16)
    location_share = band_rows * columns // time_count
    normed_two = normalize(stream).reshape(frames_here, time_count, location_share, model_width)
    allowed = frame_group[None, :] <= frame_group[:, None]
    local_projection = project(normed_two, temporal_qkv).astype(jnp.bfloat16)
    projected = lax.all_to_all(local_projection, "tm", split_axis=1, concat_axis=0, tiled=True)
    frames_all = projected.shape[0]
    location_count = projected.shape[2]
    flat = projected.reshape(frames_all, location_count, 3 * model_width)
    mixed_rows = attend(
        split_heads(flat[:, :, :model_width]),
        split_heads(flat[:, :, model_width : 2 * model_width]),
        split_heads(flat[:, :, 2 * model_width :]),
        allowed,
        "nbhd,mbhd->bhnm",
        "bhnm,mbhd->nbhd",
    )
    attended_time = mixed_rows.reshape(frames_all, 1, location_count, model_width)
    returned = lax.all_to_all(attended_time, "tm", split_axis=0, concat_axis=1, tiled=True)
    branch = project(returned.reshape(frames_here, band_rows, columns, model_width), temporal_out)
    return (stream.astype(jnp.float32) + branch).astype(jnp.bfloat16)


def solution(mesh):
    in_specs = (P("tm", "rows", None, None), P("tm"), P(), P(), P(), P(), P())
    out_specs = P("tm", "rows", None, None)
    return jax.shard_map(
        per_device, mesh=mesh, in_specs=in_specs, out_specs=out_specs, check_vma=False
    )
```

profile of v0, /device:TPU:1, one launch (start us, length us, event | category | flops | bytes accessed | tf_op | source)
XLA Modules:
  0.0 178.4 jit_solution(17099079504814936947)
XLA Ops:
  0.0 0.0 copy-start
  0.0 1.5 convert_reduce_fusion.1
  1.5 1.5 fusion.28
  3.0 3.4 %fusion.18 = bf16[1,8,64,1536]{3,2,1,0:T(8,128)(2,1)S(1)} fusion(bf16[768,2304]{1,0:T(8,128)(2,1)} %param.12, bf16[1,8,64,768]{3,2,1,0:T(8,128)(2,1)} %param.9, f32[8,64]{1,0:T(8,128)S(1)} %add_rsqrt_fusion.1, f32[8,64]{1,0:T(8,128)S(1)} %broadcast_multiply_fusion.1), kind=kOutput, calls=%fused_computation.39 | convolution fusion | flops 1210318848 | bytes 4722688 | tf_op jit(solution)/shard_map/dot_general | solution.py:35
  6.4 0.0 copy-start.1
  6.4 0.0 copy-start.2
  6.4 1.4 fusion.66
  7.8 2.5 %collective-permute-start = (bf16[1,4,64,1536]{3,2,1,0:T(8,128)(2,1)}, bf16[1,4,64,1536]{3,2,1,0:T(8,128)(2,1)}, u32[]{:S(2)}, u32[]{:S(2)}) collective-permute-start(bf16[1,4,64,1536]{3,2,1,0:T(8,128)(2,1)} %get-tuple-element.34), channel_id=1, source_target_pairs={{0,1},{1,2},{2,3},{3,4},{4,5},{5,6},{6,7},{7,0},{8,9},{9,10},{10,1... | collective-permute-start | bytes 2359304 | tf_op jit(solution)/shard_map/ppermute | solution.py:18
  10.2 3.9 %collective-permute-start.1 = (bf16[1,4,64,1536]{3,2,1,0:T(8,128)(2,1)}, bf16[1,4,64,1536]{3,2,1,0:T(8,128)(2,1)}, u32[]{:S(2)}, u32[]{:S(2)}) collective-permute-start(bf16[1,4,64,1536]{3,2,1,0:T(8,128)(2,1)} %get-tuple-element.33), channel_id=1, source_target_pairs={{1,0},{2,1},{3,2},{4,3},{5,4},{6,5},{7,6},{0,7},{9,8},{10,9},{11,1... | collective-permute-start | bytes 2359304 | tf_op jit(solution)/shard_map/ppermute | solution.py:21
  14.8 0.0 copy-done.2
  14.9 2.1 %fusion.48 = bf16[1,8,64,768]{3,2,1,0:T(8,128)(2,1)S(1)} fusion(bf16[768,2304]{1,0:T(8,128)(2,1)} %param.12, bf16[1,8,64,768]{3,2,1,0:T(8,128)(2,1)S(1)} %copy-done.2, f32[8,64]{1,0:T(8,128)S(1)} %add_rsqrt_fusion.1, f32[8,64]{1,0:T(8,128)S(1)} %broadcast_multiply_fusion.1), kind=kOutput, calls=%fused_computation.75 | convolution fusion | flops 605945856 | bytes 2756608 | tf_op jit(solution)/shard_map/dot_general | solution.py:35
  17.0 0.0 copy-done.1
  17.0 3.2 %fusion.34 = bf16[1,16,64,768]{3,2,1,0:T(8,128)(2,1)S(1)} fusion(s32[]{:T(128)} %bitcast.3, bf16[1,4,64,768]{3,2,1,0:T(8,128)(2,1)S(1)} %broadcast_in_dim.18, bf16[1,8,64,768]{3,2,1,0:T(8,128)(2,1)S(1)} %fusion.48), kind=kLoop, calls=%fused_computation.62 | loop fusion | flops 9437184 | bytes 2752516 | tf_op jit(solution)/shard_map/vmap(jit(_roll_dynamic))/concatenate | solution.py:59
  20.2 1.4 copy.41
  21.6 5.9 %reshape_reshape.2 = bf16[16,64,12,64]{3,2,1,0:T(8,128)(2,1)} reshape(bf16[1,2,8,8,8,768]{5,4,3,2,1,0:T(8,128)(2,1)} %copy.41) | data formatting | bytes 3145728 | tf_op jit(solution)/shard_map/reshape;reshape | solution.py:40
  27.5 4.2 %collective-permute-done = bf16[1,4,64,1536]{3,2,1,0:T(8,128)(2,1)} collective-permute-done((bf16[1,4,64,1536]{3,2,1,0:T(8,128)(2,1)}, bf16[1,4,64,1536]{3,2,1,0:T(8,128)(2,1)}, u32[]{:S(2)}, u32[]{:S(2)}) %collective-permute-start) | collective-permute-done | bytes 786464 | tf_op jit(solution)/shard_map/ppermute | solution.py:18
  31.7 0.0 collective-permute-done.1
  31.7 6.4 %fusion.10 = bf16[1,16,64,1536]{3,2,1,0:T(8,128)(2,1)S(1)} fusion(s32[]{:T(128)} %bitcast.3, bf16[1,4,64,1536]{3,2,1,0:T(8,128)(2,1)} %collective-permute-done, bf16[1,8,64,1536]{3,2,1,0:T(8,128)(2,1)} %copy-done.1, bf16[1,4,64,1536]{3,2,1,0:T(8,128)(2,1)} %collective-permute-done.1), kind=kLoop, calls=%fused_computation.18 | loop fusion | flops 18874368 | bytes 6291460 | tf_op jit(solution)/shard_map/vmap(jit(_roll_dynamic))/concatenate | solution.py:59
  38.1 0.3 copy.39
  38.4 2.0 %fusion.64 = (bf16[16,64,768]{2,1,0:T(8,128)(2,1)}, bf16[16,64,768]{2,1,0:T(8,128)(2,1)}) fusion(bf16[16,64,1536]{2,1,0:T(8,128)(2,1)S(1)} %bitcast.65), kind=kLoop, calls=%fused_computation.93 | loop fusion | bytes 6291456 | tf_op jit(solution)/shard_map/slice | solution.py:90
  40.5 5.9 %reshape.135 = bf16[16,64,12,64]{3,2,1,0:T(8,128)(2,1)} reshape(bf16[16,64,768]{2,1,0:T(8,128)(2,1)} %get-tuple-element.28) | data formatting | bytes 3145728 | tf_op jit(solution)/shard_map/reshape | solution.py:40
  46.4 5.2 %fusion.13 = f32[16,12,64,64]{2,3,1,0:T(8,128)S(1)} fusion(bf16[16,64,12,64]{3,2,1,0:T(8,128)(2,1)} %reshape.135, bf16[16,64,12,64]{3,2,1,0:T(8,128)(2,1)} %reshape_reshape.2), kind=kOutput, calls=%fused_computation.29 | convolution fusion | flops 100663296 | bytes 6291456 | tf_op jit(solution)/shard_map/bnhd,bmhd->bhnm/dot_general | solution.py:45
  51.6 5.1 %fusion.67 = (f32[16,12,64]{2,1,0:T(8,128)}, f32[16,12,64,64]{2,3,1,0:T(8,128)}) fusion(f32[16,12,64,64]{2,3,1,0:T(8,128)S(1)} %fusion.13), kind=kOutput, calls=%fused_computation.96 | output fusion | flops 3145791 | bytes 6340608 | tf_op jit(solution)/shard_map/sub | solution.py:49
  56.7 4.1 %copy.40 = bf16[16,64,768]{1,2,0:T(8,128)(2,1)} copy(bf16[16,64,768]{2,1,0:T(8,128)(2,1)} %get-tuple-element.29) | data formatting | bytes 3145728 | tf_op jit(solution)/shard_map/slice | solution.py:91
  60.8 6.3 %convert_bitcast_fusion = bf16[16,64,12,64]{1,3,2,0:T(8,128)(2,1)} fusion(bf16[16,64,12,64]{1,3,2,0:T(8,128)(2,1)} %bitcast.68, f32[16,12,64,64]{2,3,1,0:T(8,128)} %get-tuple-element.36, f32[16,12,64]{2,1,0:T(8,128)} %get-tuple-element.35), kind=kOutput, calls=%fused_computation.35 | convolution fusion | flops 103022592 | bytes 6340608 | tf_op jit(solution)/shard_map/bhnm,bmhd->bnhd/dot_general | solution.py:52
  67.1 6.8 %copy.45 = bf16[16,64,12,64]{3,2,1,0:T(8,128)(2,1)} copy(bf16[16,64,12,64]{1,3,2,0:T(8,128)(2,1)} %convert_bitcast_fusion) | data formatting | bytes 3145728 | tf_op jit(solution)/shard_map/convert_element_type | solution.py:53
  73.9 6.1 %reshape.136 = bf16[1,2,8,8,8,768]{5,4,3,2,1,0:T(8,128)(2,1)} reshape(bf16[16,64,12,64]{3,2,1,0:T(8,128)(2,1)} %copy.45) | data formatting | bytes 3145728 | tf_op jit(solution)/shard_map/reshape | solution.py:96
  80.0 0.0 copy-start.3
  80.0 0.0 copy-start.7
  80.0 1.7 copy.46
  81.7 0.0 copy-done.3
  81.7 0.3 copy-done.7
  82.0 1.2 convert_reduce_fusion
  83.2 0.0 copy-start.4
  83.2 0.3 fusion.26
  83.6 0.5 copy-done.4
  84.1 0.3 fusion.27
  84.3 0.0 copy-done
  84.3 3.4 %fusion.5 = bf16[1,32,16,2304]{3,2,0,1:T(8,128)(2,1)} fusion(bf16[32,16,768]{2,1,0:T(8,128)(2,1)S(1)} %bitcast.71, bf16[768,2304]{1,0:T(8,128)(2,1)S(1)} %copy-done), kind=kOutput, calls=%fused_computation.13 | convolution fusion | flops 1813118976 | bytes 6684672 | tf_op jit(solution)/shard_map/dot_general | solution.py:35
  87.7 0.0 copy-start.6
  87.7 8.5 %all-to-all-start = ((bf16[1,32,16,2304]{3,2,0,1:T(8,128)(2,1)}), bf16[1,32,16,2304]{3,2,0,1:T(8,128)(2,1)}, u32[]{:S(2)}, u32[]{:S(2)}) async-start(bf16[1,32,16,2304]{3,2,0,1:T(8,128)(2,1)} %fusion.5), calls=%async_computation | async-start | bytes 4718592 | tf_op jit(solution)/shard_map/all_to_all | solution.py:106
  96.3 0.0 copy-done.6
  96.3 0.1 broadcast_compare_fusion
  96.3 31.5 %all-to-all-done = bf16[1,32,16,2304]{3,2,0,1:T(8,128)(2,1)} async-done(((bf16[1,32,16,2304]{3,2,0,1:T(8,128)(2,1)}), bf16[1,32,16,2304]{3,2,0,1:T(8,128)(2,1)}, u32[]{:S(2)}, u32[]{:S(2)}) %all-to-all-start) | async-done | bytes 2359328 | tf_op jit(solution)/shard_map/all_to_all | solution.py:106
  127.8 3.1 %fusion.65 = (bf16[32,16,768]{2,1,0:T(8,128)(2,1)}, bf16[32,16,768]{2,1,0:T(8,128)(2,1)}, bf16[32,16,768]{2,1,0:T(8,128)(2,1)}) fusion(bf16[32,16,2304]{2,1,0:T(8,128)(2,1)} %bitcast.24), kind=kLoop, calls=%fused_computation.94 | loop fusion | bytes 4718592 | tf_op jit(solution)/shard_map/slice | solution.py:113
  130.9 3.8 %reshape.141 = bf16[32,16,12,64]{3,2,1,0:T(8,128)(2,1)} reshape(bf16[32,16,768]{2,1,0:T(8,128)(2,1)} %get-tuple-element.32) | data formatting | bytes 1572864 | tf_op jit(solution)/shard_map/reshape | solution.py:40
  134.7 3.8 %reshape.142 = bf16[32,16,12,64]{3,2,1,0:T(8,128)(2,1)} reshape(bf16[32,16,768]{2,1,0:T(8,128)(2,1)} %get-tuple-element.31) | data formatting | bytes 1572864 | tf_op jit(solution)/shard_map/reshape | solution.py:40
  138.4 3.8 %reshape.140 = bf16[32,16,12,64]{3,2,1,0:T(8,128)(2,1)} reshape(bf16[32,16,768]{2,1,0:T(8,128)(2,1)} %get-tuple-element.30) | data formatting | bytes 1572864 | tf_op jit(solution)/shard_map/reshape | solution.py:40
  142.2 4.3 %fusion.38 = f32[16,12,32,32]{2,3,1,0:T(8,128)S(1)} fusion(bf16[32,16,12,64]{3,2,1,0:T(8,128)(2,1)} %reshape.142, bf16[32,16,12,64]{3,2,1,0:T(8,128)(2,1)} %reshape.141), kind=kOutput, calls=%fused_computation.66 | convolution fusion | flops 25165824 | bytes 2359296 | tf_op jit(solution)/shard_map/nbhd,mbhd->bhnm/dot_general | solution.py:45
  146.5 0.0 copy-start.5
  146.5 1.2 fusion.68
  147.7 0.4 copy-done.5
  148.1 1.4 fusion.45
  149.5 2.0 %copy.52 = bf16[32,16,12,64]{3,2,1,0:T(8,128)(2,1)} copy(bf16[32,16,12,64]{3,0,2,1:T(8,128)(2,1)S(1)} %fusion.45) | data formatting | bytes 1572864 | tf_op jit(solution)/shard_map/convert_element_type | solution.py:53
  151.5 3.9 %reshape.143 = bf16[32,1,16,768]{3,2,0,1:T(8,128)(2,1)} reshape(bf16[32,16,12,64]{3,2,1,0:T(8,128)(2,1)} %copy.52) | data formatting | bytes 1572864 | tf_op jit(solution)/shard_map/reshape | solution.py:118
  155.4 19.8 %all_to_all.8 = bf16[32,1,16,768]{3,2,1,0:T(8,128)(2,1)S(1)} all-to-all(bf16[32,1,16,768]{3,2,1,0:T(8,128)(2,1)} %bitcast.69), channel_id=1, replica_groups=mesh['tm'=32,'rows'=8] {'tm'}, dimensions={0} | all-to-all | bytes 1572864 | tf_op jit(solution)/shard_map/all_to_all | solution.py:119
  175.2 3.1 %fusion.31 = bf16[1,8,64,768]{3,2,1,0:T(8,128)(2,1)} fusion(bf16[1,8,64,768]{3,2,1,0:T(8,128)(2,1)} %copy-done.4, bf16[8,64,768]{2,1,0:T(8,128)(2,1)S(1)} %bitcast.72, bf16[768,768]{1,0:T(8,128)(2,1)} %param.15), kind=kOutput, calls=%fused_computation.59 | convolution fusion | flops 605159424 | bytes 3538944 | tf_op jit(solution)/shard_map/dot_general | solution.py:35
  (5 shorter events, 0.0 us)
Async XLA Ops:
  0.0 84.3 %copy-start = (bf16[768,2304]{1,0:T(8,128)(2,1)S(1)}, bf16[768,2304]{1,0:T(8,128)(2,1)}, u32[]{:S(2)}) copy-start(bf16[768,2304]{1,0:T(8,128)(2,1)} %param.14) | copy-start | bytes 10616836
  6.4 10.6 %copy-start.1 = (bf16[1,8,64,1536]{3,2,1,0:T(8,128)(2,1)}, bf16[1,8,64,1536]{3,2,1,0:T(8,128)(2,1)S(1)}, u32[]{:S(2)}) copy-start(bf16[1,8,64,1536]{3,2,1,0:T(8,128)(2,1)S(1)} %fusion.18) | copy-start | bytes 4718596
  6.4 8.5 %copy-start.2 = (bf16[1,8,64,768]{3,2,1,0:T(8,128)(2,1)S(1)}, bf16[1,8,64,768]{3,2,1,0:T(8,128)(2,1)}, u32[]{:S(2)}) copy-start(bf16[1,8,64,768]{3,2,1,0:T(8,128)(2,1)} %param.9) | copy-start | bytes 2359300
  7.8 24.0 %collective-permute-start = (bf16[1,4,64,1536]{3,2,1,0:T(8,128)(2,1)}, bf16[1,4,64,1536]{3,2,1,0:T(8,128)(2,1)}, u32[]{:S(2)}, u32[]{:S(2)}) collective-permute-start(bf16[1,4,64,1536]{3,2,1,0:T(8,128)(2,1)} %get-tuple-element.34), channel_id=1, source_target_pairs={{0,1},{1,2},{2,3},{3,4},{4,5},{5,6},{6,7},{7,0},{8,9},{9,10},{10,1... | collective-permute-start | bytes 2359304 | tf_op jit(solution)/shard_map/ppermute | solution.py:18
  10.2 21.5 %collective-permute-start.1 = (bf16[1,4,64,1536]{3,2,1,0:T(8,128)(2,1)}, bf16[1,4,64,1536]{3,2,1,0:T(8,128)(2,1)}, u32[]{:S(2)}, u32[]{:S(2)}) collective-permute-start(bf16[1,4,64,1536]{3,2,1,0:T(8,128)(2,1)} %get-tuple-element.33), channel_id=1, source_target_pairs={{1,0},{2,1},{3,2},{4,3},{5,4},{6,5},{7,6},{0,7},{9,8},{10,9},{11,1... | collective-permute-start | bytes 2359304 | tf_op jit(solution)/shard_map/ppermute | solution.py:21
  80.0 1.7 copy-start.3
  80.0 2.0 %copy-start.7 = (bf16[768,768]{1,0:T(8,128)(2,1)S(1)}, bf16[768,768]{1,0:T(8,128)(2,1)}, u32[]{:S(2)}) copy-start(bf16[768,768]{1,0:T(8,128)(2,1)} %param.13) | copy-start | bytes 3538948
  83.2 0.9 copy-start.4
  87.7 8.5 %copy-start.6 = (s32[32]{0:T(128)S(1)}, s32[32]{0:T(128)}, u32[]{:S(2)}) copy-start(s32[32]{0:T(128)} %param.11) | copy-start | bytes 388
  87.7 40.1 %all-to-all-start = ((bf16[1,32,16,2304]{3,2,0,1:T(8,128)(2,1)}), bf16[1,32,16,2304]{3,2,0,1:T(8,128)(2,1)}, u32[]{:S(2)}, u32[]{:S(2)}) async-start(bf16[1,32,16,2304]{3,2,0,1:T(8,128)(2,1)} %fusion.5), calls=%async_computation | async-start | bytes 4718592 | tf_op jit(solution)/shard_map/all_to_all | solution.py:106
  146.5 1.6 copy-start.5
where the time goes:
time: 180 us; the launch traced here: 178 us
  local copies, waits for them, and re-layouts  57.1 us (32%)
  waiting for transfers between devices  35.7 us (20%)
  matrix products  30.5 us (17%)
  blocking collectives  19.8 us (11%)
  other arithmetic  19.4 us (11%)
  starting transfers between devices  14.9 us (8%)
    all_to_all x1, waiting for transfers between devices, per_device(): lax.all_to_all(local_projection, 'tm', split_axis=1, concat_axis=0, tiled...  31.5 us
    all_to_all x1, blocking collectives, per_device(): lax.all_to_all(attended_time, 'tm', split_axis=0, concat_axis=1, tiled=True)  19.8 us
    reshape x4, local copies, waits for them, and re-layouts, split_heads(): values.reshape(values.shape[:-1] + (HEADS, values.shape[-1] // HEADS))  17.2 us
    dot_general x5, matrix products, project(): product = jnp.dot(flattened, weight, preferred_element_type=jnp.float32)  13.2 us
    concatenate x2, other arithmetic, one_frame(): return jnp.roll(single_frame, direction * offset, axis=1)  9.57 us
    dot_general x2, matrix products, attend(): jnp.einsum(score_form, queries, key_rows, preferred_element_type=jnp.floa...  9.53 us
    convert_element_type x2, local copies, waits for them, and re-layouts, attend(): return mixed_rows.astype(jnp.bfloat16)  8.81 us
    all_to_all x1, starting transfers between devices, per_device(): lax.all_to_all(local_projection, 'tm', split_axis=1, concat_axis=0, tiled...  8.51 us
  transfers between devices with their start and end apart: 3, of which 2 were waited for; matrix products, arithmetic and copies ran while one was open for 7% of the time, Pallas kernels for 0%

commit v1 on v0

v1 whole, which is shorter than its diff:
```python
import jax
import jax.numpy as jnp
from jax import lax
from jax.experimental import pallas as pl
from jax.experimental.pallas import tpu as pltpu
from jax.sharding import PartitionSpec as P

D = 768
GROUP = 256
BF16 = jnp.bfloat16
F32 = jnp.float32
MESH = pl.DeviceIdType.MESH


def iota(shape, dim):
    return lax.broadcasted_iota(jnp.int32, shape, dim)


def one_hot(mask):
    return jnp.where(mask, 1.0, 0.0).astype(BF16)


def layer_norm(x):
    center = x - jnp.mean(x, axis=-1, keepdims=True)
    spread = jnp.mean(center * center, axis=-1, keepdims=True)
    return (center * lax.rsqrt(spread + 1e-05)).astype(BF16)


def dot(a, b):
    return jnp.dot(a, b, preferred_element_type=F32)


def dot_t(a, b):
    return lax.dot_general(a, b, (((1,), (1,)), ((), ())), preferred_element_type=F32)


def block_diagonal(x):
    lane = iota(x.shape, 1) // 64
    return jnp.concatenate([jnp.where(lane == h, x, jnp.zeros_like(x)) for h in range(4)], axis=0)


def spread_heads(reduce, s, fill):
    parts = []
    for half in range(2):
        part = s[:, half * 128 : half * 128 + 128]
        low = iota(part.shape, 1) < 64
        first = reduce(jnp.where(low, part, fill), axis=-1, keepdims=True)
        second = reduce(jnp.where(low, fill, part), axis=-1, keepdims=True)
        parts.append(jnp.where(low, first, second))
    return jnp.concatenate(parts, axis=1)


def attend(q, k, v, allowed):
    s = dot_t(q, block_diagonal(k))
    if allowed is not None:
        s = jnp.where(allowed, s, -1e30)
    top = spread_heads(jnp.max, s, -jnp.inf)
    e = jnp.exp((s - top) * 0.125)
    total = spread_heads(jnp.sum, e, 0.0)
    weights = (e / total).astype(BF16)
    return dot(weights, block_diagonal(v)).astype(BF16)


def kernel(
    shift_ref, group_ref, tok, wsq_h, wso_h, wtq_h, wto_h, out,
    wsq, wso, wtq, wto, town, trcv, xin, qown, qrcv, mix, sbuf, rbuf, qt, mixt, xout, obuf, mask,
    lsem, osem, zs, zr, fs, fr, bs, br,
):
    tm = lax.axis_index("tm")
    z = lax.axis_index("rows")
    core = lax.rem(tm, 2)
    x = lax.rem(tm // 2, 4)
    y = tm // 8
    column = lax.rem(tm, 8)
    zup = lax.rem(z + 1 + 6 * core, 8)
    zdown = lax.rem(z + 7 + 2 * core, 8)

    def block(i):
        return lax.rem(2 * x + 1 + i, 8)

    loads = [
        pltpu.make_async_copy(src, dst, lsem.at[n])
        for n, (src, dst) in enumerate(((wsq_h, wsq), (wso_h, wso), (wtq_h, wtq), (wto_h, wto)))
    ]

    def own_copy(i):
        return pltpu.make_async_copy(
            tok.at[pl.ds(4 - 4 * core, 4), block(i)], town.at[i], osem.at[i]
        )

    @pl.loop(0, 8)
    def _(i):
        own_copy(i).start()

    for load in loads:
        load.start()

    barrier = pltpu.get_barrier_semaphore()

    @pl.loop(1, 32)
    def _(n):
        pl.semaphore_signal(
            barrier, inc=1, device_id=(lax.rem(tm + n, 32), z), device_id_type=MESH
        )

    sender_core = y // 2
    sender_z = lax.rem(z + 7 + 2 * sender_core, 8)

    @pl.loop(0, 16)
    def _(n):
        pl.semaphore_signal(
            barrier, inc=1, device_id=(2 * n + sender_core, sender_z), device_id_type=MESH
        )

    pl.semaphore_signal(barrier, inc=1, device_id=(tm, zup), device_id_type=MESH)

    shift = shift_ref[0]

    rows, cols = iota((64, 96), 0), iota((64, 96), 1)
    gather = one_hot(
        (lax.rem(rows // 8, 4) == lax.rem(cols // 8, 4))
        & (8 * (cols // 32) + lax.rem(cols, 8) == 8 * (rows // 32) + lax.rem(rows, 8) + shift)
    )
    rows, cols = iota((128, 192), 0), iota((128, 192), 1)
    scatter = one_hot(
        (lax.rem(rows // 8, 8) == lax.rem(cols // 8, 8))
        & (8 * (rows // 64) + lax.rem(rows, 8) + 8 == 8 * (cols // 64) + lax.rem(cols, 8) + shift)
    )

    def normed_pair(buffer, t):
        parts = []
        for b in range(3):
            parts.append(buffer[lax.rem(2 * t + b, 8)].astype(F32).reshape(32, D))
        normed = layer_norm(jnp.concatenate(parts, axis=0))
        return dot(gather, normed).astype(BF16)

    @pl.loop(0, 8)
    def _(i):
        own_copy(i).wait()

    @pl.loop(0, 4)
    def _(t):
        xin[pl.ds(pl.multiple_of(t * 64, 64), 64), :] = normed_pair(town, t)

    loads[0].wait()

    def project_own(n):
        lanes = pl.ds(pl.multiple_of(n * GROUP, GROUP), GROUP)
        qown[:, lanes] = dot(xin[...], wsq[:, lanes]).astype(BF16)

    pl.loop(0, 9)(project_own)

    mix[0:64, :] = jnp.zeros((64, D), BF16)

    q_row, k_col = iota((64, 1), 0), lax.rem(iota((1, GROUP), 1), 64)

    def frame_of(n):
        m = lax.rem(n, 8)
        return (m // 2) * 8 + (n // 16) * 2 + lax.rem(m, 2)

    q_frame, k_frame = frame_of(q_row), frame_of(k_col)
    q_group, k_group = jnp.zeros_like(q_frame), jnp.zeros_like(k_frame)
    for f in range(32):
        value = group_ref[f]
        q_group = jnp.where(q_frame == f, value, q_group)
        k_group = jnp.where(k_frame == f, value, k_group)
    same = lax.rem(q_row // 8, 2) == lax.rem(k_col // 8, 2)
    mask[...] = jnp.where(same & (k_group <= q_group), 1, 0)

    pl.semaphore_wait(barrier, 48)

    def z_copy(i):
        return pltpu.make_async_remote_copy(
            src_ref=tok.at[pl.ds(4 * core, 4), block(i)],
            dst_ref=trcv.at[i],
            send_sem=zs.at[i],
            recv_sem=zr.at[i],
            device_id=(tm, zdown),
            device_id_type=MESH,
        )

    @pl.loop(0, 8)
    def _(i):
        z_copy(i).start()

    for load in loads[1:]:
        load.wait()

    def forward(i, h, u, act):
        half = core if h else 1 - core
        target = (2 * half + u) * 8 + block(i)
        target_z = zup if h else z
        source = sbuf.at[i, h, pl.ds(2 * u, 2)]
        place = rbuf.at[x, 2 * y + core]
        number = i * 4 + h * 2 + u
        remote = pltpu.make_async_remote_copy(
            src_ref=source,
            dst_ref=place,
            send_sem=fs.at[number],
            recv_sem=fr.at[x],
            device_id=(target, target_z),
            device_id_type=MESH,
        )
        if h:
            act(remote, None)
        else:
            here = target == tm

            @pl.when(here)
            def _():
                act(None, pltpu.make_async_copy(source, place, fr.at[x]))

            @pl.when(jnp.logical_not(here))
            def _():
                act(remote, None)

    def start(remote, local):
        (remote if local is None else local).start()

    def finish(remote, local):
        if local is None:
            remote.wait_send()

    def send_block(i):
        for h in range(2):
            for u in range(2):
                forward(i, h, u, start)

    def finish_blocks(first, count, mixed, matrix):
        flat = dot(matrix, mixed).astype(BF16)
        y_out = dot(flat, wso[...])
        residual = []
        for n in range(count):
            for buffer in (town, trcv):
                residual.append(buffer[first + n].astype(F32).reshape(32, D))
        stream = (jnp.concatenate(residual, axis=0) + y_out).astype(BF16)
        for n in range(count):
            for h in range(2):
                at = (2 * n + h) * 32
                for r in range(4):
                    sbuf[first + n, h, r] = stream[at + 8 * r : at + 8 * r + 8, :]

    z_copy(0).wait_recv()

    @pl.loop(0, 4)
    def _(t):
        z_copy(2 * t + 1).wait_recv()

        @pl.when(t < 3)
        def _():
            z_copy(2 * t + 2).wait_recv()

        received = normed_pair(trcv, t)
        for n in range(9):
            lanes = slice(n * GROUP, n * GROUP + GROUP)
            qrcv[:, lanes] = dot(received, wsq[:, lanes]).astype(BF16)
        for w in range(2):
            own_rows = pl.ds(pl.multiple_of(t * 64 + w * 32, 32), 32)
            for g in range(3):

                def part(n):
                    lanes = slice(n * D + g * GROUP, n * D + g * GROUP + GROUP)
                    return jnp.concatenate(
                        [qown[own_rows, lanes], qrcv[w * 32 : w * 32 + 32, lanes]], axis=0
                    )

                mixed = attend(part(0), part(1), part(2), None)
                at = pl.ds(pl.multiple_of((2 * t + w + 1) * 64, 64), 64)
                mix[at, g * GROUP : g * GROUP + GROUP] = mixed
        recent = mix[pl.ds(pl.multiple_of(t * 128, 128), 192), :]
        finish_blocks(2 * t, 2, recent, scatter)

        @pl.when(t > 0)
        def _():
            send_block(2 * t)

        send_block(2 * t + 1)

    edge = jnp.concatenate([mix[512:576, :], mix[64:128, :]], axis=0)
    finish_blocks(0, 1, edge, scatter[:64, :128])
    send_block(0)

    rows, cols = iota((128, 128), 0), iota((128, 128), 1)
    regroup = one_hot((rows // 8 == lax.rem(cols, 16)) & (lax.rem(rows, 8) == cols // 16))
    rows, cols = iota((64, 64), 0), iota((64, 64), 1)
    swap = one_hot((rows // 8 == lax.rem(cols, 8)) & (lax.rem(rows, 8) == cols // 8))

    @pl.loop(0, 4)
    def _(n):
        source = lax.rem(x + 3 - n, 4)
        pltpu.make_async_copy(rbuf.at[source], rbuf.at[source], fr.at[source]).wait()
        normed = layer_norm(rbuf[source].astype(F32).reshape(128, D))
        ordered = dot(regroup, normed).astype(BF16)
        for m in range(9):
            lanes = slice(m * GROUP, m * GROUP + GROUP)
            qt[source, :, lanes] = dot(ordered, wtq[:, lanes]).astype(BF16)

    def give_back(r, source, m, act):
        target = (m // 2) * 8 + source * 2 + lax.rem(m, 2)
        data = obuf.at[r, source, m]
        place = out.at[2 * y + r, column]
        here = target == tm

        @pl.when(here)
        def _():
            act(None, pltpu.make_async_copy(data, place, br))

        @pl.when(jnp.logical_not(here))
        def _():
            act(
                pltpu.make_async_remote_copy(
                    src_ref=data,
                    dst_ref=place,
                    send_sem=bs.at[r * 32 + source * 8 + m],
                    recv_sem=br,
                    device_id=(target, z),
                    device_id_type=MESH,
                ),
                None,
            )

    @pl.loop(0, 2)
    def _(r):
        @pl.loop(0, 2)
        def _(pair):
            for lp in range(2):
                at = pl.ds(pl.multiple_of(r * 64 + pair * 32 + lp * 16, 16), 16)
                for g in range(3):

                    def part(n):
                        lanes = slice(n * D + g * GROUP, n * D + g * GROUP + GROUP)
                        return jnp.concatenate([qt[s, at, lanes] for s in range(4)], axis=0)

                    mixed = attend(part(0), part(1), part(2), mask[...] != 0)
                    for s in range(4):
                        mixt[s, at, g * GROUP : g * GROUP + GROUP] = mixed[s * 16 : s * 16 + 16, :]

        for s in range(4):
            half = mixt[s, pl.ds(pl.multiple_of(r * 64, 64), 64), :]
            xout[s * 64 : s * 64 + 64, :] = dot(swap, half).astype(BF16)
        for n in range(3):
            lanes = slice(n * GROUP, n * GROUP + GROUP)
            branch = dot(xout[...], wto[:, lanes])
            residual = rbuf[:, :, r, :, lanes].astype(F32).reshape(256, GROUP)
            obuf[r, :, :, :, lanes] = (residual + branch).reshape(4, 8, 8, GROUP).astype(BF16)

        @pl.loop(0, 4)
        def _(n):
            source = lax.rem(x + 1 + n, 4)

            @pl.loop(0, 8)
            def _(m):
                give_back(r, source, m, start)

    pltpu.make_async_copy(out, out, br).wait()

    @pl.loop(0, 8)
    def _(i):
        z_copy(i).wait_send()
        for h in range(2):
            for u in range(2):
                forward(i, h, u, finish)

    @pl.loop(0, 2)
    def _(r):
        @pl.loop(0, 4)
        def _(s):
            @pl.loop(0, 8)
            def _(m):
                give_back(r, s, m, finish)


def per_device(
    tokens, col_shift, frame_group, spatial_qkv, spatial_out, temporal_qkv, temporal_out
):
    smem = pl.BlockSpec(memory_space=pltpu.SMEM)
    anywhere = pl.BlockSpec(memory_space=pl.ANY)
    dma = pltpu.SemaphoreType.DMA
    result = pl.pallas_call(
        kernel,
        out_shape=jax.ShapeDtypeStruct((8, 8, 8, D), BF16),
        in_specs=[smem, smem] + [anywhere] * 5,
        out_specs=anywhere,
        scratch_shapes=[
            pltpu.VMEM((D, 3 * D), BF16),
            pltpu.VMEM((D, D), BF16),
            pltpu.VMEM((D, 3 * D), BF16),
            pltpu.VMEM((D, D), BF16),
            pltpu.VMEM((8, 4, 8, D), BF16),
            pltpu.VMEM((8, 4, 8, D), BF16),
            pltpu.VMEM((256, D), BF16),
            pltpu.VMEM((256, 3 * D), BF16),
            pltpu.VMEM((64, 3 * D), BF16),
            pltpu.VMEM((576, D), BF16),
            pltpu.VMEM((8, 2, 4, 8, D), BF16),
            pltpu.VMEM((4, 8, 2, 8, D), BF16),
            pltpu.VMEM((4, 128, 3 * D), BF16),
            pltpu.VMEM((4, 128, D), BF16),
            pltpu.VMEM((256, D), BF16),
            pltpu.VMEM((2, 4, 8, 8, D), BF16),
            pltpu.VMEM((64, GROUP), jnp.int32),
            dma((4,)),
            dma((8,)),
            dma((8,)),
            dma((8,)),
            dma((32,)),
            dma((4,)),
            dma((64,)),
            dma,
        ],
        compiler_params=pltpu.CompilerParams(
            collective_id=0, has_side_effects=True, vmem_limit_bytes=56 * 1024 * 1024
        ),
    )(
        col_shift,
        frame_group,
        tokens.reshape(8, 8, 8, D),
        spatial_qkv,
        spatial_out,
        temporal_qkv,
        temporal_out,
    )
    return result.reshape(tokens.shape)


def solution(mesh):
    in_specs = (P("tm", "rows", None, None), P("tm"), P(), P(), P(), P(), P())
    out_specs = P("tm", "rows", None, None)
    return jax.shard_map(
        per_device, mesh=mesh, in_specs=in_specs, out_specs=out_specs, check_vma=False
    )
```

time: 180 us -> 62.1 us (0.35)
  Pallas kernels: 0 us -> 59.2 us
  local copies, waits for them, and re-layouts: 57.1 us -> 2.06 us
  waiting for transfers between devices: 35.7 us -> 0 us
  matrix products: 30.5 us -> 0 us
  blocking collectives: 19.8 us -> 0 us
  other arithmetic: 19.4 us -> 0 us
  starting transfers between devices: 14.9 us -> 0 us
    pallas_call x0 -> x1, Pallas kernels: none -> 59.2 us  [per_device(): pl.pallas_call(kernel, out_shape=jax.ShapeDtypeStruct((8, 8, 8, D), BF16)...]
    all_to_all x1 -> x0, waiting for transfers between devices: 31.5 us -> none  [per_device(): lax.all_to_all(local_projection, 'tm', split_axis=1, concat_axis=0, tiled...]
    dot_general x9 -> x0, matrix products: 30.5 us -> none  [the longest x5 13.2 us: project(): product = jnp.dot(flattened, weight, preferred_element_type=jnp.float32)]
    reshape x6 -> x0, local copies, waits for them, and re-layouts: 27.2 us -> none  [the longest x4 17.2 us: split_heads(): values.reshape(values.shape[:-1] + (HEADS, values.shape[-1] // HEADS))]
    all_to_all x1 -> x0, blocking collectives: 19.8 us -> none  [per_device(): lax.all_to_all(attended_time, 'tm', split_axis=0, concat_axis=1, tiled=True)]
    slice x4 -> x0, local copies, waits for them, and re-layouts: 10.6 us -> none  [the longest x1 4.13 us: per_device(): pair_windows[:, :, model_width:]]
    concatenate x2 -> x0, other arithmetic: 9.57 us -> none  [one_frame(): return jnp.roll(single_frame, direction * offset, axis=1)]
    convert_element_type x2 -> x0, local copies, waits for them, and re-layouts: 8.81 us -> none  [attend(): return mixed_rows.astype(jnp.bfloat16)]
  transfers between devices with their start and end apart: 3 -> 0, of which waited for: 2 -> 0; matrix products, arithmetic and copies ran while one was open for 7% -> 0% of each run, Pallas kernels for 0% -> 0%
where the time goes in v1:
time: 62.1 us; the launch traced here: 61.9 us
  Pallas kernels  59.2 us (95%)
  local copies, waits for them, and re-layouts  2.06 us (3%)
  between operations  0.66 us (1%)
    pallas_call x1, Pallas kernels, per_device(): pl.pallas_call(kernel, out_shape=jax.ShapeDtypeStruct((8, 8, 8, D), BF16)...  59.2 us
    unnamed x1, local copies, waits for them, and re-layouts  2.06 us

profile of v1, /device:TPU:1, one launch (start us, length us, event | category | flops | bytes accessed | tf_op | source)
XLA Modules:
  0.0 61.9 jit_solution(4575607877618923642)
XLA Ops:
  0.7 59.2 %shard_map.73 = bf16[8,8,8,768]{3,2,1,0:T(8,128)(2,1)} custom-call(s32[1]{0:T(128)S(6)} %copy.9.shift_ref, s32[32]{0:T(128)} %group_ref.1, bf16[8,8,8,768]{3,2,1,0:T(8,128)(2,1)} %bitcast.3, bf16[768,2304]{1,0:T(8,128)(2,1)} %wsq_h.1, bf16[768,768]{1,0:T(8,128)(2,1)} %wso_h.1, bf16[768,2304]{1,0:T(8,128)(2,1)} %wtq_h.1, bf16[768,768]{1,0:T(8,128)(2,1)} %wto_h.1), custom_call_target="tpu_custom_call" | custom-call | tf_op jit(solution)/shard_map/pallas_call | solution.py:379
  59.8 2.1 %copy.10 = bf16[1,8,64,768]{3,2,1,0:T(8,128)(2,1)} copy(bf16[1,8,64,768]{3,2,1,0:T(8,128)(2,1)} %bitcast.2) | data formatting | bytes 1572864

commit v2 on v1

v2 whole, which is shorter than its diff:
```python
import jax
import jax.numpy as jnp
from jax import lax
from jax.experimental import pallas as pl
from jax.experimental.pallas import tpu as pltpu
from jax.sharding import PartitionSpec as P

D = 768
GROUP = 256
BF16 = jnp.bfloat16
F32 = jnp.float32
MESH = pl.DeviceIdType.MESH
AHEAD = 2
BEHIND = 2


def iota(shape, dim):
    return lax.broadcasted_iota(jnp.int32, shape, dim)


def one_hot(mask):
    return jnp.where(mask, 1.0, 0.0).astype(BF16)


def layer_norm(x):
    center = x - jnp.mean(x, axis=-1, keepdims=True)
    spread = jnp.mean(center * center, axis=-1, keepdims=True)
    return (center * lax.rsqrt(spread + 1e-05)).astype(BF16)


def dot(a, b):
    return jnp.dot(a, b, preferred_element_type=F32)


def dot_t(a, b):
    return lax.dot_general(a, b, (((1,), (1,)), ((), ())), preferred_element_type=F32)


def block_diagonal(x):
    lane = iota(x.shape, 1) // 64
    return jnp.concatenate([jnp.where(lane == h, x, jnp.zeros_like(x)) for h in range(4)], axis=0)


def attend(s):
    e = jnp.exp((s - jnp.max(s, axis=0, keepdims=True)) * 0.125)
    return (e * (1.0 / jnp.sum(e, axis=0, keepdims=True))).astype(BF16)


def attend_all(bodies, allowed, same_head):
    def scores(body):
        s = dot_t(body[1](), block_diagonal(body[0]()))
        return s if allowed is None else jnp.where(allowed, s, -1e30)

    waiting, ready = [scores(body) for body in bodies[:AHEAD]], []
    for n, body in enumerate(bodies):
        if n + AHEAD < len(bodies):
            waiting.append(scores(bodies[n + AHEAD]))
        ready.append(attend(waiting[n]))
        if n >= BEHIND:
            mix_values(ready[n - BEHIND], *bodies[n - BEHIND][2:], same_head)
    for n in range(len(bodies) - BEHIND, len(bodies)):
        mix_values(ready[n], *bodies[n][2:], same_head)


def mix_values(weights, values, slot, store, same_head):
    values = values()
    blank = jnp.zeros_like(weights)
    padded = jnp.concatenate([blank, weights] if slot else [weights, blank], axis=0)
    for p in range(2):
        lanes = slice(p * 128, p * 128 + 128)
        mixed = dot(values[lanes, :], padded[:, lanes])
        store(p, jnp.where(same_head, mixed, 0.0).astype(BF16))


def kernel(
    shift_ref, group_ref, tok, wsq_h, wso_h, wtq_h, wto_h, out,
    wsq, wso, wtq, wto, wsv, wtv, town, trcv, xin, qown, qrcv, values, mix, sbuf, rbuf, normed_t, qt,
    mixt, xout, obuf, mask, lsem, osem, zs, zr, fs, fr, bs, br,
):
    tm = lax.axis_index("tm")
    z = lax.axis_index("rows")
    core = lax.rem(tm, 2)
    x = lax.rem(tm // 2, 4)
    y = tm // 8
    column = lax.rem(tm, 8)
    zup = lax.rem(z + 1 + 6 * core, 8)
    zdown = lax.rem(z + 7 + 2 * core, 8)

    def block(i):
        return lax.rem(2 * x + 1 + i, 8)

    loads = [
        pltpu.make_async_copy(src, dst, lsem.at[n])
        for n, (src, dst) in enumerate(((wsq_h, wsq), (wso_h, wso), (wtq_h, wtq), (wto_h, wto)))
    ]

    def own_copy(i):
        return pltpu.make_async_copy(
            tok.at[pl.ds(4 - 4 * core, 4), block(i)], town.at[i], osem.at[i]
        )

    @pl.loop(0, 8)
    def _(i):
        own_copy(i).start()

    for load in loads:
        load.start()

    barrier = pltpu.get_barrier_semaphore()

    @pl.loop(1, 32)
    def _(n):
        pl.semaphore_signal(
            barrier, inc=1, device_id=(lax.rem(tm + n, 32), z), device_id_type=MESH
        )

    sender_core = y // 2
    sender_z = lax.rem(z + 7 + 2 * sender_core, 8)

    @pl.loop(0, 16)
    def _(n):
        pl.semaphore_signal(
            barrier, inc=1, device_id=(2 * n + sender_core, sender_z), device_id_type=MESH
        )

    pl.semaphore_signal(barrier, inc=1, device_id=(tm, zup), device_id_type=MESH)

    shift = shift_ref[0]

    rows, cols = iota((64, 96), 0), iota((64, 96), 1)
    gather = one_hot(
        (lax.rem(rows // 8, 4) == lax.rem(cols // 8, 4))
        & (8 * (cols // 32) + lax.rem(cols, 8) == 8 * (rows // 32) + lax.rem(rows, 8) + shift)
    )
    rows, cols = iota((128, 384), 0), iota((128, 384), 1)
    scatter = one_hot(
        (lax.rem(rows // 8, 8) == lax.rem(cols // 8, 8))
        & (8 * (rows // 64) + lax.rem(rows, 8) + 8 == 8 * (cols // 128) + lax.rem(cols, 8) + shift)
    )
    same_head = iota((128, 128), 0) // 64 == iota((128, 128), 1) // 64
    unit = one_hot(iota((GROUP, GROUP), 0) == iota((GROUP, GROUP), 1))

    def transpose_values(weight, result):
        @pl.loop(0, 3)
        def _(i):
            rows_out = pl.ds(pl.multiple_of(i * GROUP, GROUP), GROUP)
            lanes = pl.ds(pl.multiple_of(2 * D + i * GROUP, GROUP), GROUP)
            for j in range(3):
                part = slice(j * GROUP, j * GROUP + GROUP)
                result[rows_out, part] = dot_t(unit, weight[part, lanes]).astype(BF16)

    def normed_pair(buffer, t):
        parts = []
        for b in range(3):
            parts.append(buffer[lax.rem(2 * t + b, 8)].astype(F32).reshape(32, D))
        normed = layer_norm(jnp.concatenate(parts, axis=0))
        return dot(gather, normed).astype(BF16)

    @pl.loop(0, 8)
    def _(i):
        own_copy(i).wait()

    @pl.loop(0, 4)
    def _(t):
        xin[pl.ds(pl.multiple_of(t * 64, 64), 64), :] = normed_pair(town, t)

    loads[0].wait()

    def project_own(n):
        lanes = pl.ds(pl.multiple_of(n * GROUP, GROUP), GROUP)
        qown[:, lanes] = dot(xin[...], wsq[:, lanes]).astype(BF16)

    pl.loop(0, 6)(project_own)
    transpose_values(wsq, wsv)

    for p in range(6):
        mix[p, :, 0:128] = jnp.zeros((128, 128), BF16)

    k_row, q_col = iota((64, 1), 0), lax.rem(iota((1, GROUP), 1), 64)

    def frame_of(n):
        m = lax.rem(n, 8)
        return (m // 2) * 8 + (n // 16) * 2 + lax.rem(m, 2)

    k_frame, q_frame = frame_of(k_row), frame_of(q_col)
    q_group, k_group = jnp.zeros_like(q_frame), jnp.zeros_like(k_frame)
    for f in range(32):
        value = group_ref[f]
        q_group = jnp.where(q_frame == f, value, q_group)
        k_group = jnp.where(k_frame == f, value, k_group)
    same = lax.rem(k_row // 8, 2) == lax.rem(q_col // 8, 2)
    mask[...] = jnp.where(same & (k_group <= q_group), 1, 0)

    pl.semaphore_wait(barrier, 48)

    def z_copy(i):
        return pltpu.make_async_remote_copy(
            src_ref=tok.at[pl.ds(4 * core, 4), block(i)],
            dst_ref=trcv.at[i],
            send_sem=zs,
            recv_sem=zr.at[i],
            device_id=(tm, zdown),
            device_id_type=MESH,
        )

    @pl.loop(0, 8)
    def _(i):
        z_copy(i).start()

    for load in loads[1:]:
        load.wait()
    transpose_values(wtq, wtv)

    def send_block(i):
        for h in range(2):
            for u in range(2):
                half = core if h else 1 - core
                target = (2 * half + u) * 8 + block(i)
                source = sbuf.at[i * 4 + h * 2 + u]
                place = rbuf.at[x, 2 * y + core]
                remote = pltpu.make_async_remote_copy(
                    src_ref=source,
                    dst_ref=place,
                    send_sem=fs,
                    recv_sem=fr.at[x],
                    device_id=(target, zup if h else z),
                    device_id_type=MESH,
                )
                if h:
                    remote.start()
                else:
                    here = target == tm

                    @pl.when(here)
                    def _():
                        pltpu.make_async_copy(source, place, fr.at[x]).start()

                    pl.when(jnp.logical_not(here))(remote.start)

    def finish_blocks(first, count, mixed, matrix):
        flat = jnp.concatenate([dot_t(matrix, part).astype(BF16) for part in mixed], axis=1)
        y_out = dot(flat, wso[...])
        residual = []
        for n in range(count):
            for buffer in (town, trcv):
                residual.append(buffer[first + n].astype(F32).reshape(32, D))
        stream = (jnp.concatenate(residual, axis=0) + y_out).astype(BF16)
        for n in range(count):
            for h in range(2):
                at = (2 * n + h) * 32
                for r in range(4):
                    chunk = (first + n) * 4 + h * 2 + r // 2
                    sbuf[chunk, r % 2] = stream[at + 8 * r : at + 8 * r + 8, :]

    z_copy(0).wait_recv()

    @pl.loop(0, 4)
    def _(t):
        z_copy(2 * t + 1).wait_recv()

        @pl.when(t < 3)
        def _():
            z_copy(2 * t + 2).wait_recv()

        received = normed_pair(trcv, t)
        own_pair = xin[pl.ds(pl.multiple_of(t * 64, 64), 64), :]
        pair = jnp.concatenate(
            [own_pair[:32], received[:32], own_pair[32:], received[32:]], axis=0
        )
        for n in range(3):
            part_rows = slice(n * GROUP, n * GROUP + GROUP)
            values[part_rows, :] = dot_t(wsv[part_rows, :], pair).astype(BF16)
        for n in range(6):
            lanes = slice(n * GROUP, n * GROUP + GROUP)
            qrcv[:, lanes] = dot(received, wsq[:, lanes]).astype(BF16)
        def window(w, g):
            own_rows = pl.ds(pl.multiple_of(t * 64 + w * 32, 32), 32)

            def part(n):
                lanes = slice(n * D + g * GROUP, n * D + g * GROUP + GROUP)
                return jnp.concatenate(
                    [qown[own_rows, lanes], qrcv[w * 32 : w * 32 + 32, lanes]], axis=0
                )

            def store(p, mixed):
                at = pl.ds(pl.multiple_of((2 * t + w + 1) * 128, 128), 128)
                mix[2 * g + p, :, at] = mixed

            def group_values():
                return values[g * GROUP : g * GROUP + GROUP, :]

            return lambda: part(0), lambda: part(1), group_values, w, store

        attend_all([window(w, g) for w in range(2) for g in range(3)], None, same_head)
        last_three = pl.ds(pl.multiple_of(t * 256, 256), 384)
        recent = [mix[p, :, last_three] for p in range(6)]
        finish_blocks(2 * t, 2, recent, scatter)

        @pl.when(t > 0)
        def _():
            send_block(2 * t)

        send_block(2 * t + 1)

    edge = [jnp.concatenate([mix[p, :, 1024:1152], mix[p, :, 128:256]], axis=1) for p in range(6)]
    finish_blocks(0, 1, edge, scatter[:64, :256])
    send_block(0)

    rows, cols = iota((128, 128), 0), iota((128, 128), 1)
    regroup = one_hot((rows // 8 == lax.rem(cols, 16)) & (lax.rem(rows, 8) == cols // 16))
    rows, cols = iota((256, 512), 0), iota((256, 512), 1)
    swap = one_hot(
        (rows // 64 == lax.rem(cols // 16, 4))
        & (lax.rem(rows // 8, 8) == lax.rem(cols, 8))
        & (lax.rem(rows, 8) == 2 * (cols // 128) + lax.rem(cols // 8, 2))
    )

    @pl.loop(0, 4)
    def _(n):
        source = lax.rem(x + 3 - n, 4)
        pltpu.make_async_copy(rbuf.at[source], rbuf.at[source], fr.at[source]).wait()
        normed = layer_norm(rbuf[source].astype(F32).reshape(128, D))
        ordered = dot(regroup, normed).astype(BF16)
        normed_t[source] = ordered
        for m in range(6):
            lanes = slice(m * GROUP, m * GROUP + GROUP)
            qt[source, :, lanes] = dot(ordered, wtq[:, lanes]).astype(BF16)

    @pl.loop(0, 2)
    def _(r):
        @pl.loop(0, 2)
        def _(pair):
            def at(lp):
                return pl.ds(pl.multiple_of(r * 64 + pair * 32 + lp * 16, 16), 16)

            tokens_pair = jnp.concatenate(
                [normed_t[s, at(lp), :] for lp in range(2) for s in range(4)], axis=0
            )
            for n in range(3):
                part_rows = slice(n * GROUP, n * GROUP + GROUP)
                values[part_rows, :] = dot_t(wtv[part_rows, :], tokens_pair).astype(BF16)
            def location(lp, g):
                def part(n):
                    lanes = slice(n * D + g * GROUP, n * D + g * GROUP + GROUP)
                    return jnp.concatenate([qt[s, at(lp), lanes] for s in range(4)], axis=0)

                def store(p, mixed):
                    place = pl.ds(pl.multiple_of((2 * pair + lp) * 128, 128), 128)
                    mixt[2 * g + p, :, place] = mixed

                def group_values():
                    return values[g * GROUP : g * GROUP + GROUP, :]

                return lambda: part(0), lambda: part(1), group_values, lp, store

            bodies = [location(lp, g) for lp in range(2) for g in range(3)]
            attend_all(bodies, mask[...] != 0, same_head)

        for p in range(6):
            xout[:, p * 128 : p * 128 + 128] = dot_t(swap, mixt[p]).astype(BF16)
        for n in range(3):
            lanes = slice(n * GROUP, n * GROUP + GROUP)
            branch = dot(xout[...], wto[:, lanes])
            residual = rbuf[:, :, r, :, lanes].astype(F32).reshape(256, GROUP)
            result = (residual + branch).astype(BF16)
            for k in range(32):
                frame = (k % 8) // 2 * 8 + k // 8 * 2 + k % 2
                obuf[r * 32 + frame, :, lanes] = result[k * 8 : k * 8 + 8, :]

        place = out.at[2 * y + r, column]

        @pl.loop(1, 32)
        def _(n):
            target = lax.rem(tm + n, 32)
            pltpu.make_async_remote_copy(
                src_ref=obuf.at[r * 32 + target],
                dst_ref=place,
                send_sem=bs,
                recv_sem=br,
                device_id=(target, z),
                device_id_type=MESH,
            ).start()

        pltpu.make_async_copy(obuf.at[r * 32 + tm], place, br).start()

    def wait_bytes(ref, sem):
        pltpu.make_async_copy(ref, ref, sem).wait()

    wait_bytes(out, br)
    wait_bytes(trcv, zs)
    local = y // 2 == 1 - core

    @pl.when(local)
    def _():
        wait_bytes(sbuf.at[pl.ds(0, 31)], fs)

    @pl.when(jnp.logical_not(local))
    def _():
        wait_bytes(sbuf, fs)

    wait_bytes(obuf.at[pl.ds(0, 62)], bs)


def per_device(
    tokens, col_shift, frame_group, spatial_qkv, spatial_out, temporal_qkv, temporal_out
):
    smem = pl.BlockSpec(memory_space=pltpu.SMEM)
    anywhere = pl.BlockSpec(memory_space=pl.ANY)
    dma = pltpu.SemaphoreType.DMA
    result = pl.pallas_call(
        kernel,
        out_shape=jax.ShapeDtypeStruct((8, 8, 8, D), BF16),
        in_specs=[smem, smem] + [anywhere] * 5,
        out_specs=anywhere,
        scratch_shapes=[
            pltpu.VMEM((D, 3 * D), BF16),
            pltpu.VMEM((D, D), BF16),
            pltpu.VMEM((D, 3 * D), BF16),
            pltpu.VMEM((D, D), BF16),
            pltpu.VMEM((D, D), BF16),
            pltpu.VMEM((D, D), BF16),
            pltpu.VMEM((8, 4, 8, D), BF16),
            pltpu.VMEM((8, 4, 8, D), BF16),
            pltpu.VMEM((256, D), BF16),
            pltpu.VMEM((256, 2 * D), BF16),
            pltpu.VMEM((64, 2 * D), BF16),
            pltpu.VMEM((D, 128), BF16),
            pltpu.VMEM((6, 128, 9 * 128), BF16),
            pltpu.VMEM((32, 2, 8, D), BF16),
            pltpu.VMEM((4, 8, 2, 8, D), BF16),
            pltpu.VMEM((4, 128, D), BF16),
            pltpu.VMEM((4, 128, 2 * D), BF16),
            pltpu.VMEM((6, 128, 512), BF16),
            pltpu.VMEM((256, D), BF16),
            pltpu.VMEM((64, 8, D), BF16),
            pltpu.VMEM((64, GROUP), jnp.int32),
            dma((4,)),
            dma((8,)),
            dma,
            dma((8,)),
            dma,
            dma((4,)),
            dma,
            dma,
        ],
        compiler_params=pltpu.CompilerParams(
            collective_id=0, has_side_effects=True, vmem_limit_bytes=56 * 1024 * 1024
        ),
    )(
        col_shift,
        frame_group,
        tokens.reshape(8, 8, 8, D),
        spatial_qkv,
        spatial_out,
        temporal_qkv,
        temporal_out,
    )
    return result.reshape(tokens.shape)


def solution(mesh):
    in_specs = (P("tm", "rows", None, None), P("tm"), P(), P(), P(), P(), P())
    out_specs = P("tm", "rows", None, None)
    return jax.shard_map(
        per_device, mesh=mesh, in_specs=in_specs, out_specs=out_specs, check_vma=False
    )
```

time: 62.1 us -> 52.2 us (0.84)
  Pallas kernels: 59.2 us -> 49.3 us
    pallas_call x1, Pallas kernels: 59.2 us -> 49.3 us  [per_device(): pl.pallas_call(kernel, out_shape=jax.ShapeDtypeStruct((8, 8, 8, D), BF16)...]
where the time goes in v2:
time: 52.2 us; the launch traced here: 52 us
  Pallas kernels  49.3 us (94%)
  local copies, waits for them, and re-layouts  2.06 us (4%)
  between operations  0.66 us (1%)
    pallas_call x1, Pallas kernels, per_device(): pl.pallas_call(kernel, out_shape=jax.ShapeDtypeStruct((8, 8, 8, D), BF16)...  49.3 us
    unnamed x1, local copies, waits for them, and re-layouts  2.06 us

profile of v2, /device:TPU:1, one launch (start us, length us, event | category | flops | bytes accessed | tf_op | source)
XLA Modules:
  0.0 52.0 jit_solution(5340484167182272405)
XLA Ops:
  0.7 49.3 %shard_map.73 = bf16[8,8,8,768]{3,2,1,0:T(8,128)(2,1)} custom-call(s32[1]{0:T(128)S(6)} %copy.9.shift_ref, s32[32]{0:T(128)} %group_ref.1, bf16[8,8,8,768]{3,2,1,0:T(8,128)(2,1)} %bitcast.3, bf16[768,2304]{1,0:T(8,128)(2,1)} %wsq_h.1, bf16[768,768]{1,0:T(8,128)(2,1)} %wso_h.1, bf16[768,2304]{1,0:T(8,128)(2,1)} %wtq_h.1, bf16[768,768]{1,0:T(8,128)(2,1)} %wto_h.1), custom_call_target="tpu_custom_call" | custom-call | tf_op jit(solution)/shard_map/pallas_call | solution.py:410
  50.0 2.1 %copy.10 = bf16[1,8,64,768]{3,2,1,0:T(8,128)(2,1)} copy(bf16[1,8,64,768]{3,2,1,0:T(8,128)(2,1)} %bitcast.2) | data formatting | bytes 1572864

commit v3 on v2

--- a/solution.py
+++ b/solution.py
@@ -1,3 +1,5 @@
+import functools
+
 import jax
 import jax.numpy as jnp
 from jax import lax
@@ -46,7 +48,9 @@
     return (e * (1.0 / jnp.sum(e, axis=0, keepdims=True))).astype(BF16)
 
 
-def attend_all(bodies, allowed, same_head):
+def attend_all(bodies, allowed, same_head, extra=()):
+    extra = list(extra)
+    share = -(-len(extra) // len(bodies))
     def scores(body):
         s = dot_t(body[1](), block_diagonal(body[0]()))
         return s if allowed is None else jnp.where(allowed, s, -1e30)
@@ -58,6 +62,8 @@
         ready.append(attend(waiting[n]))
         if n >= BEHIND:
             mix_values(ready[n - BEHIND], *bodies[n - BEHIND][2:], same_head)
+        for work in extra[n * share : n * share + share]:
+            work()
     for n in range(len(bodies) - BEHIND, len(bodies)):
         mix_values(ready[n], *bodies[n][2:], same_head)
 
@@ -103,10 +109,11 @@
     def _(i):
         own_copy(i).start()
 
-    for load in loads:
-        load.start()
+    loads[0].start()
+    loads[1].start()
 
     barrier = pltpu.get_barrier_semaphore()
+    pl.semaphore_signal(barrier, inc=1, device_id=(tm, zup), device_id_type=MESH)
 
     @pl.loop(1, 32)
     def _(n):
@@ -122,8 +129,6 @@
         pl.semaphore_signal(
             barrier, inc=1, device_id=(2 * n + sender_core, sender_z), device_id_type=MESH
         )
-
-    pl.semaphore_signal(barrier, inc=1, device_id=(tm, zup), device_id_type=MESH)
 
     shift = shift_ref[0]
 
@@ -152,7 +157,7 @@
     def normed_pair(buffer, t):
         parts = []
         for b in range(3):
-            parts.append(buffer[lax.rem(2 * t + b, 8)].astype(F32).reshape(32, D))
+            parts.append(buffer[(2 * t + b) % 8 if isinstance(t, int) else lax.rem(2 * t + b, 8)].astype(F32).reshape(32, D))
         normed = layer_norm(jnp.concatenate(parts, axis=0))
         return dot(gather, normed).astype(BF16)
 
@@ -163,33 +168,6 @@
     @pl.loop(0, 4)
     def _(t):
         xin[pl.ds(pl.multiple_of(t * 64, 64), 64), :] = normed_pair(town, t)
-
-    loads[0].wait()
-
-    def project_own(n):
-        lanes = pl.ds(pl.multiple_of(n * GROUP, GROUP), GROUP)
-        qown[:, lanes] = dot(xin[...], wsq[:, lanes]).astype(BF16)
-
-    pl.loop(0, 6)(project_own)
-    transpose_values(wsq, wsv)
-
-    for p in range(6):
-        mix[p, :, 0:128] = jnp.zeros((128, 128), BF16)
-
-    k_row, q_col = iota((64, 1), 0), lax.rem(iota((1, GROUP), 1), 64)
-
-    def frame_of(n):
-        m = lax.rem(n, 8)
-        return (m // 2) * 8 + (n // 16) * 2 + lax.rem(m, 2)
-
-    k_frame, q_frame = frame_of(k_row), frame_of(q_col)
-    q_group, k_group = jnp.zeros_like(q_frame), jnp.zeros_like(k_frame)
-    for f in range(32):
-        value = group_ref[f]
-        q_group = jnp.where(q_frame == f, value, q_group)
-        k_group = jnp.where(k_frame == f, value, k_group)
-    same = lax.rem(k_row // 8, 2) == lax.rem(q_col // 8, 2)
-    mask[...] = jnp.where(same & (k_group <= q_group), 1, 0)
 
     pl.semaphore_wait(barrier, 48)
 
@@ -207,9 +185,36 @@
     def _(i):
         z_copy(i).start()
 
-    for load in loads[1:]:
-        load.wait()
-    transpose_values(wtq, wtv)
+    loads[0].wait()
+    loads[2].start()
+    loads[3].start()
+
+    def project_own(n):
+        lanes = pl.ds(pl.multiple_of(n * GROUP, GROUP), GROUP)
+        qown[:, lanes] = dot(xin[...], wsq[:, lanes]).astype(BF16)
+
+    pl.loop(0, 6)(project_own)
+    transpose_values(wsq, wsv)
+
+    for p in range(6):
+        mix[p, :, 0:128] = jnp.zeros((128, 128), BF16)
+
+    k_row, q_col = iota((64, 1), 0), lax.rem(iota((1, GROUP), 1), 64)
+
+    def frame_of(n):
+        m = lax.rem(n, 8)
+        return (m // 2) * 8 + (n // 16) * 2 + lax.rem(m, 2)
+
+    k_frame, q_frame = frame_of(k_row), frame_of(q_col)
+    q_group, k_group = jnp.zeros_like(q_frame), jnp.zeros_like(k_frame)
+    for f in range(32):
+        value = group_ref[f]
+        q_group = jnp.where(q_frame == f, value, q_group)
+        k_group = jnp.where(k_frame == f, value, k_group)
+    same = lax.rem(k_row // 8, 2) == lax.rem(q_col // 8, 2)
+    mask[...] = jnp.where(same & (k_group <= q_group), 1, 0)
+
+    loads[1].wait()
 
     def send_block(i):
         for h in range(2):
@@ -226,7 +231,7 @@
                     device_id=(target, zup if h else z),
                     device_id_type=MESH,
                 )
-                if h:
+                if h or 0 < i < 7:
                     remote.start()
                 else:
                     here = target == tm
@@ -252,59 +257,69 @@
                     chunk = (first + n) * 4 + h * 2 + r // 2
                     sbuf[chunk, r % 2] = stream[at + 8 * r : at + 8 * r + 8, :]
 
-    z_copy(0).wait_recv()
-
-    @pl.loop(0, 4)
-    def _(t):
-        z_copy(2 * t + 1).wait_recv()
-
-        @pl.when(t < 3)
-        def _():
-            z_copy(2 * t + 2).wait_recv()
-
-        received = normed_pair(trcv, t)
-        own_pair = xin[pl.ds(pl.multiple_of(t * 64, 64), 64), :]
-        pair = jnp.concatenate(
-            [own_pair[:32], received[:32], own_pair[32:], received[32:]], axis=0
-        )
-        for n in range(3):
+    def front(t):
+        slot, pair = t % 2, []
+
+        def norm():
+            received = normed_pair(trcv, t)
+            own_pair = xin[t * 64 : t * 64 + 64, :]
+            pair.append(received)
+            pair.append(
+                jnp.concatenate(
+                    [own_pair[:32], received[:32], own_pair[32:], received[32:]], axis=0
+                )
+            )
+
+        def project(n):
+            lanes = slice(n * GROUP, n * GROUP + GROUP)
+            qrcv[slot, :, lanes] = dot(pair[0], wsq[:, lanes]).astype(BF16)
+
+        def project_values(n):
             part_rows = slice(n * GROUP, n * GROUP + GROUP)
-            values[part_rows, :] = dot_t(wsv[part_rows, :], pair).astype(BF16)
-        for n in range(6):
-            lanes = slice(n * GROUP, n * GROUP + GROUP)
-            qrcv[:, lanes] = dot(received, wsq[:, lanes]).astype(BF16)
-        def window(w, g):
-            own_rows = pl.ds(pl.multiple_of(t * 64 + w * 32, 32), 32)
-
-            def part(n):
-                lanes = slice(n * D + g * GROUP, n * D + g * GROUP + GROUP)
-                return jnp.concatenate(
-                    [qown[own_rows, lanes], qrcv[w * 32 : w * 32 + 32, lanes]], axis=0
-                )
-
-            def store(p, mixed):
-                at = pl.ds(pl.multiple_of((2 * t + w + 1) * 128, 128), 128)
-                mix[2 * g + p, :, at] = mixed
-
-            def group_values():
-                return values[g * GROUP : g * GROUP + GROUP, :]
-
-            return lambda: part(0), lambda: part(1), group_values, w, store
-
-        attend_all([window(w, g) for w in range(2) for g in range(3)], None, same_head)
-        last_three = pl.ds(pl.multiple_of(t * 256, 256), 384)
-        recent = [mix[p, :, last_three] for p in range(6)]
+            values[slot, part_rows, :] = dot_t(wsv[part_rows, :], pair[1]).astype(BF16)
+
+        work = [norm] + [functools.partial(project, n) for n in (0, 3, 1, 4, 2, 5)]
+        return work + [functools.partial(project_values, n) for n in range(3)]
+
+    def window(t, w, g):
+        own_rows = slice(t * 64 + w * 32, t * 64 + w * 32 + 32)
+
+        def part(n):
+            lanes = slice(n * D + g * GROUP, n * D + g * GROUP + GROUP)
+            received = qrcv[t % 2, w * 32 : w * 32 + 32, lanes]
+            return jnp.concatenate([qown[own_rows, lanes], received], axis=0)
+
+        def store(p, mixed):
+            at = (2 * t + w + 1) * 128
+            mix[2 * g + p, :, at : at + 128] = mixed
+
+        def group_values():
+            return values[t % 2, g * GROUP : g * GROUP + GROUP, :]
+
+        return lambda: part(0), lambda: part(1), group_values, w, store
+
+    for i in range(3):
+        z_copy(i).wait_recv()
+    for work in front(0):
+        work()
+    for t in range(4):
+        for i in range(2 * t + 3, min(2 * t + 5, 8)):
+            z_copy(i).wait_recv()
+        bodies = [window(t, w, g) for w in range(2) for g in range(3)]
+        attend_all(bodies, None, same_head, front(t + 1) if t < 3 else ())
+        recent = [mix[p, :, t * 256 : t * 256 + 384] for p in range(6)]
         finish_blocks(2 * t, 2, recent, scatter)
-
-        @pl.when(t > 0)
-        def _():
+        if t:
             send_block(2 * t)
-
         send_block(2 * t + 1)
 
     edge = [jnp.concatenate([mix[p, :, 1024:1152], mix[p, :, 128:256]], axis=1) for p in range(6)]
     finish_blocks(0, 1, edge, scatter[:64, :256])
     send_block(0)
+
+    loads[2].wait()
+    loads[3].wait()
+    transpose_values(wtq, wtv)
 
     rows, cols = iota((128, 128), 0), iota((128, 128), 1)
     regroup = one_hot((rows // 8 == lax.rem(cols, 16)) & (lax.rem(rows, 8) == cols // 16))
@@ -326,38 +341,36 @@
             lanes = slice(m * GROUP, m * GROUP + GROUP)
             qt[source, :, lanes] = dot(ordered, wtq[:, lanes]).astype(BF16)
 
-    @pl.loop(0, 2)
-    def _(r):
-        @pl.loop(0, 2)
-        def _(pair):
-            def at(lp):
-                return pl.ds(pl.multiple_of(r * 64 + pair * 32 + lp * 16, 16), 16)
-
+    def at(q, lp):
+        return slice(q * 32 + lp * 16, q * 32 + lp * 16 + 16)
+
+    def later(q):
+        def project_values(n):
             tokens_pair = jnp.concatenate(
-                [normed_t[s, at(lp), :] for lp in range(2) for s in range(4)], axis=0
+                [normed_t[s, at(q, lp), :] for lp in range(2) for s in range(4)], axis=0
             )
-            for n in range(3):
-                part_rows = slice(n * GROUP, n * GROUP + GROUP)
-                values[part_rows, :] = dot_t(wtv[part_rows, :], tokens_pair).astype(BF16)
-            def location(lp, g):
-                def part(n):
-                    lanes = slice(n * D + g * GROUP, n * D + g * GROUP + GROUP)
-                    return jnp.concatenate([qt[s, at(lp), lanes] for s in range(4)], axis=0)
-
-                def store(p, mixed):
-                    place = pl.ds(pl.multiple_of((2 * pair + lp) * 128, 128), 128)
-                    mixt[2 * g + p, :, place] = mixed
-
-                def group_values():
-                    return values[g * GROUP : g * GROUP + GROUP, :]
-
-                return lambda: part(0), lambda: part(1), group_values, lp, store
-
-            bodies = [location(lp, g) for lp in range(2) for g in range(3)]
-            attend_all(bodies, mask[...] != 0, same_head)
-
+            part_rows = slice(n * GROUP, n * GROUP + GROUP)
+            values[q % 2, part_rows, :] = dot_t(wtv[part_rows, :], tokens_pair).astype(BF16)
+
+        return [functools.partial(project_values, n) for n in range(3)]
+
+    def location(q, lp, g):
+        def part(n):
+            lanes = slice(n * D + g * GROUP, n * D + g * GROUP + GROUP)
+            return jnp.concatenate([qt[s, at(q, lp), lanes] for s in range(4)], axis=0)
+
+        def store(p, mixed):
+            place = (2 * (q % 2) + lp) * 128
+            mixt[q // 2, 2 * g + p, :, place : place + 128] = mixed
+
+        def group_values():
+            return values[q % 2, g * GROUP : g * GROUP + GROUP, :]
+
+        return lambda: part(0), lambda: part(1), group_values, lp, store
+
+    def give_back(r):
         for p in range(6):
-            xout[:, p * 128 : p * 128 + 128] = dot_t(swap, mixt[p]).astype(BF16)
+            xout[:, p * 128 : p * 128 + 128] = dot_t(swap, mixt[r, p]).astype(BF16)
         for n in range(3):
             lanes = slice(n * GROUP, n * GROUP + GROUP)
             branch = dot(xout[...], wto[:, lanes])
@@ -383,6 +396,14 @@
 
         pltpu.make_async_copy(obuf.at[r * 32 + tm], place, br).start()
 
+    for work in later(0):
+        work()
+    for q in range(4):
+        bodies = [location(q, lp, g) for lp in range(2) for g in range(3)]
+        attend_all(bodies, mask[...] != 0, same_head, later(q + 1) if q < 3 else ())
+        if q % 2:
+            give_back(q // 2)
+
     def wait_bytes(ref, sem):
         pltpu.make_async_copy(ref, ref, sem).wait()
 
@@ -399,6 +420,12 @@
         wait_bytes(sbuf, fs)
 
     wait_bytes(obuf.at[pl.ds(0, 62)], bs)
+
+
+def write_out(result, out, sem):
+    copy = pltpu.make_async_copy(result, out, sem)
+    copy.start()
+    copy.wait()
 
 
 def per_device(
@@ -409,9 +436,9 @@
     dma = pltpu.SemaphoreType.DMA
     result = pl.pallas_call(
         kernel,
-        out_shape=jax.ShapeDtypeStruct((8, 8, 8, D), BF16),
+        out_shape=pltpu.VMEM((8, 8, 8, D), BF16),
         in_specs=[smem, smem] + [anywhere] * 5,
-        out_specs=anywhere,
+        out_specs=pl.BlockSpec(memory_space=pltpu.VMEM),
         scratch_shapes=[
             pltpu.VMEM((D, 3 * D), BF16),
             pltpu.VMEM((D, D), BF16),
@@ -423,14 +450,14 @@
             pltpu.VMEM((8, 4, 8, D), BF16),
             pltpu.VMEM((256, D), BF16),
             pltpu.VMEM((256, 2 * D), BF16),
-            pltpu.VMEM((64, 2 * D), BF16),
-            pltpu.VMEM((D, 128), BF16),
+            pltpu.VMEM((2, 64, 2 * D), BF16),
+            pltpu.VMEM((2, D, 128), BF16),
             pltpu.VMEM((6, 128, 9 * 128), BF16),
             pltpu.VMEM((32, 2, 8, D), BF16),
             pltpu.VMEM((4, 8, 2, 8, D), BF16),
             pltpu.VMEM((4, 128, D), BF16),
             pltpu.VMEM((4, 128, 2 * D), BF16),
-            pltpu.VMEM((6, 128, 512), BF16),
+            pltpu.VMEM((2, 6, 128, 512), BF16),
             pltpu.VMEM((256, D), BF16),
             pltpu.VMEM((64, 8, D), BF16),
             pltpu.VMEM((64, GROUP), jnp.int32),
@@ -455,7 +482,14 @@
         temporal_qkv,
         temporal_out,
     )
-    return result.reshape(tokens.shape)
+    written = pl.pallas_call(
+        write_out,
+        out_shape=jax.ShapeDtypeStruct((8, 8, 8, D), BF16),
+        in_specs=[anywhere],
+        out_specs=anywhere,
+        scratch_shapes=[dma],
+    )(pltpu.with_memory_space_constraint(result, pltpu.VMEM))
+    return written.reshape(tokens.shape)
 
 
 def solution(mesh):

time: 52.2 us -> 49.9 us (0.956)
  local copies, waits for them, and re-layouts: 2.06 us -> 0 us
    unnamed x1 -> x0, local copies, waits for them, and re-layouts: 2.06 us -> none
    pallas_call x1 -> x2, Pallas kernels: 49.3 us -> 49 us  [the longest x1 48.1 us: per_device(): pl.pallas_call(kernel, out_shape=pltpu.VMEM((8, 8, 8, D), BF16), in_specs...]
where the time goes in v3:
time: 49.9 us
  Pallas kernels  49 us (98%)
  between operations  0.82 us (2%)
    pallas_call x1, Pallas kernels, per_device(): pl.pallas_call(kernel, out_shape=pltpu.VMEM((8, 8, 8, D), BF16), in_specs...  48.1 us

profile of v3, /device:TPU:1, one launch (start us, length us, event | category | flops | bytes accessed | tf_op | source)
XLA Modules:
  0.0 49.9 jit_solution(18306084512494262239)
XLA Ops:
  0.7 48.1 %shard_map.73.result = bf16[8,8,8,768]{3,2,1,0:T(8,128)(2,1)S(1)} custom-call(s32[1]{0:T(128)S(6)} %copy.8.shift_ref, s32[32]{0:T(128)} %group_ref.1, bf16[8,8,8,768]{3,2,1,0:T(8,128)(2,1)} %bitcast.2, bf16[768,2304]{1,0:T(8,128)(2,1)} %wsq_h.1, bf16[768,768]{1,0:T(8,128)(2,1)} %wso_h.1, bf16[768,2304]{1,0:T(8,128)(2,1)} %wtq_h.1, bf16[768,768]{1,0:T(8,128)(2,1)} %wto_h.1), custom_call_target="tpu_custom_call" | custom-call | tf_op jit(solution)/shard_map/pallas_call | solution.py:437
  48.8 0.9 %shard_map.74 = bf16[8,8,8,768]{3,2,1,0:T(8,128)(2,1)} custom-call(bf16[8,8,8,768]{3,2,1,0:T(8,128)(2,1)S(1)} %shard_map.73.result), custom_call_target="tpu_custom_call" | custom-call | tf_op jit(solution)/shard_map/pallas_call | solution.py:485

commit v4 on v3

--- a/solution.py
+++ b/solution.py
@@ -88,12 +88,8 @@
     core = lax.rem(tm, 2)
     x = lax.rem(tm // 2, 4)
     y = tm // 8
-    column = lax.rem(tm, 8)
     zup = lax.rem(z + 1 + 6 * core, 8)
     zdown = lax.rem(z + 7 + 2 * core, 8)
-
-    def block(i):
-        return lax.rem(2 * x + 1 + i, 8)
 
     loads = [
         pltpu.make_async_copy(src, dst, lsem.at[n])
@@ -102,7 +98,7 @@
 
     def own_copy(i):
         return pltpu.make_async_copy(
-            tok.at[pl.ds(4 - 4 * core, 4), block(i)], town.at[i], osem.at[i]
+            tok.at[pl.ds(4 - 4 * core, 4), i], town.at[i], osem.at[i]
         )
 
     @pl.loop(0, 8)
@@ -145,14 +141,12 @@
     same_head = iota((128, 128), 0) // 64 == iota((128, 128), 1) // 64
     unit = one_hot(iota((GROUP, GROUP), 0) == iota((GROUP, GROUP), 1))
 
-    def transpose_values(weight, result):
-        @pl.loop(0, 3)
-        def _(i):
-            rows_out = pl.ds(pl.multiple_of(i * GROUP, GROUP), GROUP)
-            lanes = pl.ds(pl.multiple_of(2 * D + i * GROUP, GROUP), GROUP)
-            for j in range(3):
-                part = slice(j * GROUP, j * GROUP + GROUP)
-                result[rows_out, part] = dot_t(unit, weight[part, lanes]).astype(BF16)
+    def transpose_values(weight, result, i):
+        rows_out = slice(i * GROUP, i * GROUP + GROUP)
+        lanes = slice(2 * D + i * GROUP, 2 * D + i * GROUP + GROUP)
+        for j in range(3):
+            part = slice(j * GROUP, j * GROUP + GROUP)
+            result[rows_out, part] = dot_t(unit, weight[part, lanes]).astype(BF16)
 
     def normed_pair(buffer, t):
         parts = []
@@ -173,7 +167,7 @@
 
     def z_copy(i):
         return pltpu.make_async_remote_copy(
-            src_ref=tok.at[pl.ds(4 * core, 4), block(i)],
+            src_ref=tok.at[pl.ds(4 * core, 4), i],
             dst_ref=trcv.at[i],
             send_sem=zs,
             recv_sem=zr.at[i],
@@ -194,7 +188,8 @@
         qown[:, lanes] = dot(xin[...], wsq[:, lanes]).astype(BF16)
 
     pl.loop(0, 6)(project_own)
-    transpose_values(wsq, wsv)
+    for i in range(3):
+        transpose_values(wsq, wsv, i)
 
     for p in range(6):
         mix[p, :, 0:128] = jnp.zeros((128, 128), BF16)
@@ -216,31 +211,40 @@
 
     loads[1].wait()
 
+    own_row = 2 * y + x // 2
+
     def send_block(i):
-        for h in range(2):
-            for u in range(2):
-                half = core if h else 1 - core
-                target = (2 * half + u) * 8 + block(i)
-                source = sbuf.at[i * 4 + h * 2 + u]
-                place = rbuf.at[x, 2 * y + core]
-                remote = pltpu.make_async_remote_copy(
-                    src_ref=source,
-                    dst_ref=place,
-                    send_sem=fs,
-                    recv_sem=fr.at[x],
-                    device_id=(target, zup if h else z),
-                    device_id_type=MESH,
-                )
-                if h or 0 < i < 7:
-                    remote.start()
-                else:
-                    here = target == tm
-
-                    @pl.when(here)
-                    def _():
-                        pltpu.make_async_copy(source, place, fr.at[x]).start()
-
-                    pl.when(jnp.logical_not(here))(remote.start)
+        number = (i + 7) % 8
+        r, side, low = number // 4, number // 2 % 2, number % 2
+        place = rbuf.at[r, x, 2 * y + core]
+
+        def send(h, row):
+            half = core if h else 1 - core
+            p = 4 * half + row
+            target = ((p // 2) * 4 + 2 * lax.rem(p, 2) + low) * 2 + side
+            return pltpu.make_async_remote_copy(
+                src_ref=sbuf.at[i * 8 + h * 4 + row],
+                dst_ref=place,
+                send_sem=fs,
+                recv_sem=fr.at[r],
+                device_id=(target, zup if h else z),
+                device_id_type=MESH,
+            )
+
+        for row in range(4):
+            send(1, row).start()
+        mine = lax.rem(own_row, 4)
+        for n in range(1, 4):
+            send(0, lax.rem(mine + n, 4)).start()
+        here = (y // 2 == 1 - core) & (core == side) & (lax.rem(x, 2) == low)
+
+        @pl.when(here)
+        def _():
+            pltpu.make_async_copy(sbuf.at[i * 8 + mine], place, fr.at[r]).start()
+
+        @pl.when(jnp.logical_not(here))
+        def _():
+            send(0, mine).start()
 
     def finish_blocks(first, count, mixed, matrix):
         flat = jnp.concatenate([dot_t(matrix, part).astype(BF16) for part in mixed], axis=1)
@@ -254,8 +258,7 @@
             for h in range(2):
                 at = (2 * n + h) * 32
                 for r in range(4):
-                    chunk = (first + n) * 4 + h * 2 + r // 2
-                    sbuf[chunk, r % 2] = stream[at + 8 * r : at + 8 * r + 8, :]
+                    sbuf[(first + n) * 8 + h * 4 + r] = stream[at + 8 * r : at + 8 * r + 8, :]
 
     def front(t):
         slot, pair = t % 2, []
@@ -306,7 +309,12 @@
         for i in range(2 * t + 3, min(2 * t + 5, 8)):
             z_copy(i).wait_recv()
         bodies = [window(t, w, g) for w in range(2) for g in range(3)]
-        attend_all(bodies, None, same_head, front(t + 1) if t < 3 else ())
+        if t < 3:
+            extra = front(t + 1)
+        else:
+            loads[2].wait()
+            extra = [functools.partial(transpose_values, wtq, wtv, i) for i in range(3)]
+        attend_all(bodies, None, same_head, extra)
         recent = [mix[p, :, t * 256 : t * 256 + 384] for p in range(6)]
         finish_blocks(2 * t, 2, recent, scatter)
         if t:
@@ -317,12 +325,13 @@
     finish_blocks(0, 1, edge, scatter[:64, :256])
     send_block(0)
 
-    loads[2].wait()
     loads[3].wait()
-    transpose_values(wtq, wtv)
-
-    rows, cols = iota((128, 128), 0), iota((128, 128), 1)
-    regroup = one_hot((rows // 8 == lax.rem(cols, 16)) & (lax.rem(rows, 8) == cols // 16))
+    rows, cols = iota((256, 256), 0), iota((256, 256), 1)
+    regroup = one_hot(
+        (rows // 64 == cols // 64)
+        & (lax.rem(rows // 8, 8) == lax.rem(cols, 8))
+        & (lax.rem(rows, 8) == lax.rem(cols // 8, 8))
+    )
     rows, cols = iota((256, 512), 0), iota((256, 512), 1)
     swap = one_hot(
         (rows // 64 == lax.rem(cols // 16, 4))
@@ -330,24 +339,25 @@
         & (lax.rem(rows, 8) == 2 * (cols // 128) + lax.rem(cols // 8, 2))
     )
 
-    @pl.loop(0, 4)
-    def _(n):
-        source = lax.rem(x + 3 - n, 4)
-        pltpu.make_async_copy(rbuf.at[source], rbuf.at[source], fr.at[source]).wait()
-        normed = layer_norm(rbuf[source].astype(F32).reshape(128, D))
-        ordered = dot(regroup, normed).astype(BF16)
-        normed_t[source] = ordered
+    def wait_bytes(ref, sem):
+        pltpu.make_async_copy(ref, ref, sem).wait()
+
+    def project_half(r):
+        wait_bytes(rbuf.at[r], fr.at[r])
+        normed = layer_norm(rbuf[r].astype(F32).reshape(256, D))
+        normed_t[r] = dot(regroup, normed).astype(BF16)
         for m in range(6):
             lanes = slice(m * GROUP, m * GROUP + GROUP)
-            qt[source, :, lanes] = dot(ordered, wtq[:, lanes]).astype(BF16)
-
-    def at(q, lp):
-        return slice(q * 32 + lp * 16, q * 32 + lp * 16 + 16)
+            qt[r, :, lanes] = dot(normed_t[r], wtq[:, lanes]).astype(BF16)
+
+    def at(q, lp, s):
+        first = s * 64 + q % 2 * 32 + lp * 16
+        return slice(first, first + 16)
 
     def later(q):
         def project_values(n):
             tokens_pair = jnp.concatenate(
-                [normed_t[s, at(q, lp), :] for lp in range(2) for s in range(4)], axis=0
+                [normed_t[q // 2, at(q, lp, s), :] for lp in range(2) for s in range(4)], axis=0
             )
             part_rows = slice(n * GROUP, n * GROUP + GROUP)
             values[q % 2, part_rows, :] = dot_t(wtv[part_rows, :], tokens_pair).astype(BF16)
@@ -357,7 +367,7 @@
     def location(q, lp, g):
         def part(n):
             lanes = slice(n * D + g * GROUP, n * D + g * GROUP + GROUP)
-            return jnp.concatenate([qt[s, at(q, lp), lanes] for s in range(4)], axis=0)
+            return jnp.concatenate([qt[q // 2, at(q, lp, s), lanes] for s in range(4)], axis=0)
 
         def store(p, mixed):
             place = (2 * (q % 2) + lp) * 128
@@ -374,13 +384,13 @@
         for n in range(3):
             lanes = slice(n * GROUP, n * GROUP + GROUP)
             branch = dot(xout[...], wto[:, lanes])
-            residual = rbuf[:, :, r, :, lanes].astype(F32).reshape(256, GROUP)
+            residual = rbuf[r, :, :, :, lanes].astype(F32).reshape(256, GROUP)
             result = (residual + branch).astype(BF16)
             for k in range(32):
                 frame = (k % 8) // 2 * 8 + k // 8 * 2 + k % 2
                 obuf[r * 32 + frame, :, lanes] = result[k * 8 : k * 8 + 8, :]
 
-        place = out.at[2 * y + r, column]
+        place = out.at[own_row, lax.rem(r * 4 + core * 2 + lax.rem(x, 2) + 1, 8)]
 
         @pl.loop(1, 32)
         def _(n):
@@ -396,16 +406,15 @@
 
         pltpu.make_async_copy(obuf.at[r * 32 + tm], place, br).start()
 
-    for work in later(0):
-        work()
     for q in range(4):
+        if q % 2 == 0:
+            project_half(q // 2)
+            for work in later(q):
+                work()
         bodies = [location(q, lp, g) for lp in range(2) for g in range(3)]
-        attend_all(bodies, mask[...] != 0, same_head, later(q + 1) if q < 3 else ())
+        attend_all(bodies, mask[...] != 0, same_head, () if q % 2 else later(q + 1))
         if q % 2:
             give_back(q // 2)
-
-    def wait_bytes(ref, sem):
-        pltpu.make_async_copy(ref, ref, sem).wait()
 
     wait_bytes(out, br)
     wait_bytes(trcv, zs)
@@ -413,7 +422,7 @@
 
     @pl.when(local)
     def _():
-        wait_bytes(sbuf.at[pl.ds(0, 31)], fs)
+        wait_bytes(sbuf.at[pl.ds(0, 62)], fs)
 
     @pl.when(jnp.logical_not(local))
     def _():
@@ -453,10 +462,10 @@
             pltpu.VMEM((2, 64, 2 * D), BF16),
             pltpu.VMEM((2, D, 128), BF16),
             pltpu.VMEM((6, 128, 9 * 128), BF16),
-            pltpu.VMEM((32, 2, 8, D), BF16),
-            pltpu.VMEM((4, 8, 2, 8, D), BF16),
-            pltpu.VMEM((4, 128, D), BF16),
-            pltpu.VMEM((4, 128, 2 * D), BF16),
+            pltpu.VMEM((64, 8, D), BF16),
+            pltpu.VMEM((2, 4, 8, 8, D), BF16),
+            pltpu.VMEM((2, 256, D), BF16),
+            pltpu.VMEM((2, 256, 2 * D), BF16),
             pltpu.VMEM((2, 6, 128, 512), BF16),
             pltpu.VMEM((256, D), BF16),
             pltpu.VMEM((64, 8, D), BF16),
@@ -466,7 +475,7 @@
             dma,
             dma((8,)),
             dma,
-            dma((4,)),
+            dma((2,)),
             dma,
             dma,
         ],

time: 49.9 us -> 44.6 us (0.89)
  Pallas kernels: 49 us -> 43.6 us
    pallas_call x1, Pallas kernels: 48.1 us -> 42.8 us  [per_device(): pl.pallas_call(kernel, out_shape=pltpu.VMEM((8, 8, 8, D), BF16), in_specs...]
where the time goes in v4:
time: 44.6 us; the launch traced here: 44.5 us
  Pallas kernels  43.6 us (98%)
  between operations  0.82 us (2%)
    pallas_call x1, Pallas kernels, per_device(): pl.pallas_call(kernel, out_shape=pltpu.VMEM((8, 8, 8, D), BF16), in_specs...  42.8 us

profile of v4, /device:TPU:1, one launch (start us, length us, event | category | flops | bytes accessed | tf_op | source)
XLA Modules:
  0.0 44.5 jit_solution(3008626025013209750)
XLA Ops:
  0.7 42.8 %shard_map.73.result = bf16[8,8,8,768]{3,2,1,0:T(8,128)(2,1)S(1)} custom-call(s32[1]{0:T(128)S(6)} %copy.8.shift_ref, s32[32]{0:T(128)} %group_ref.1, bf16[8,8,8,768]{3,2,1,0:T(8,128)(2,1)} %bitcast.2, bf16[768,2304]{1,0:T(8,128)(2,1)} %wsq_h.1, bf16[768,768]{1,0:T(8,128)(2,1)} %wso_h.1, bf16[768,2304]{1,0:T(8,128)(2,1)} %wtq_h.1, bf16[768,768]{1,0:T(8,128)(2,1)} %wto_h.1), custom_call_target="tpu_custom_call" | custom-call | tf_op jit(solution)/shard_map/pallas_call | solution.py:446
  43.4 0.9 %shard_map.74 = bf16[8,8,8,768]{3,2,1,0:T(8,128)(2,1)} custom-call(bf16[8,8,8,768]{3,2,1,0:T(8,128)(2,1)S(1)} %shard_map.73.result), custom_call_target="tpu_custom_call" | custom-call | tf_op jit(solution)/shard_map/pallas_call | solution.py:494

commit v5 on v4

--- a/solution.py
+++ b/solution.py
@@ -14,6 +14,9 @@
 MESH = pl.DeviceIdType.MESH
 AHEAD = 2
 BEHIND = 2
+FAR_FIRST = [(dy, dx, dc) for dy in (2, 1, 3, 0) for dx in (2, 1, 3, 0) for dc in (0, 1)]
+FAR_FIRST.remove((0, 0, 0))
+FAR_FIRST.sort(key=lambda d: -min(d[0], 4 - d[0]) - min(d[1], 4 - d[1]))
 
 
 def iota(shape, dim):
@@ -91,6 +94,9 @@
     zup = lax.rem(z + 1 + 6 * core, 8)
     zdown = lax.rem(z + 7 + 2 * core, 8)
 
+    barrier = pltpu.get_barrier_semaphore()
+    pl.semaphore_signal(barrier, inc=1, device_id=(tm, zup), device_id_type=MESH)
+
     loads = [
         pltpu.make_async_copy(src, dst, lsem.at[n])
         for n, (src, dst) in enumerate(((wsq_h, wsq), (wso_h, wso), (wtq_h, wtq), (wto_h, wto)))
@@ -106,10 +112,6 @@
         own_copy(i).start()
 
     loads[0].start()
-    loads[1].start()
-
-    barrier = pltpu.get_barrier_semaphore()
-    pl.semaphore_signal(barrier, inc=1, device_id=(tm, zup), device_id_type=MESH)
 
     @pl.loop(1, 32)
     def _(n):
@@ -180,8 +182,8 @@
         z_copy(i).start()
 
     loads[0].wait()
-    loads[2].start()
-    loads[3].start()
+    for load in loads[1:]:
+        load.start()
 
     def project_own(n):
         lanes = pl.ds(pl.multiple_of(n * GROUP, GROUP), GROUP)
@@ -194,20 +196,21 @@
     for p in range(6):
         mix[p, :, 0:128] = jnp.zeros((128, 128), BF16)
 
-    k_row, q_col = iota((64, 1), 0), lax.rem(iota((1, GROUP), 1), 64)
-
-    def frame_of(n):
-        m = lax.rem(n, 8)
-        return (m // 2) * 8 + (n // 16) * 2 + lax.rem(m, 2)
-
-    k_frame, q_frame = frame_of(k_row), frame_of(q_col)
-    q_group, k_group = jnp.zeros_like(q_frame), jnp.zeros_like(k_frame)
-    for f in range(32):
-        value = group_ref[f]
-        q_group = jnp.where(q_frame == f, value, q_group)
-        k_group = jnp.where(k_frame == f, value, k_group)
-    same = lax.rem(k_row // 8, 2) == lax.rem(q_col // 8, 2)
-    mask[...] = jnp.where(same & (k_group <= q_group), 1, 0)
+    def build_mask():
+        k_row, q_col = iota((64, 1), 0), lax.rem(iota((1, GROUP), 1), 64)
+
+        def frame_of(n):
+            m = lax.rem(n, 8)
+            return (m // 2) * 8 + (n // 16) * 2 + lax.rem(m, 2)
+
+        k_frame, q_frame = frame_of(k_row), frame_of(q_col)
+        q_group, k_group = jnp.zeros_like(q_frame), jnp.zeros_like(k_frame)
+        for f in range(32):
+            value = group_ref[f]
+            q_group = jnp.where(q_frame == f, value, q_group)
+            k_group = jnp.where(k_frame == f, value, k_group)
+        same = lax.rem(k_row // 8, 2) == lax.rem(q_col // 8, 2)
+        mask[...] = jnp.where(same & (k_group <= q_group), 1, 0)
 
     loads[1].wait()
 
@@ -314,6 +317,7 @@
         else:
             loads[2].wait()
             extra = [functools.partial(transpose_values, wtq, wtv, i) for i in range(3)]
+            extra.append(build_mask)
         attend_all(bodies, None, same_head, extra)
         recent = [mix[p, :, t * 256 : t * 256 + 384] for p in range(6)]
         finish_blocks(2 * t, 2, recent, scatter)
@@ -392,9 +396,8 @@
 
         place = out.at[own_row, lax.rem(r * 4 + core * 2 + lax.rem(x, 2) + 1, 8)]
 
-        @pl.loop(1, 32)
-        def _(n):
-            target = lax.rem(tm + n, 32)
+        for dy, dx, dc in FAR_FIRST:
+            target = (lax.rem(y + dy, 4) * 4 + lax.rem(x + dx, 4)) * 2 + lax.rem(core + dc, 2)
             pltpu.make_async_remote_copy(
                 src_ref=obuf.at[r * 32 + target],
                 dst_ref=place,

time: 44.6 us -> 44.7 us (level)
  no operation moved by 1% of the time
where the time goes in v5:
time: 44.7 us; the launch traced here: 44.6 us
  Pallas kernels  43.8 us (98%)
  between operations  0.82 us (2%)
    pallas_call x1, Pallas kernels, per_device(): pl.pallas_call(kernel, out_shape=pltpu.VMEM((8, 8, 8, D), BF16), in_specs...  42.9 us

profile of v5, /device:TPU:1, one launch (start us, length us, event | category | flops | bytes accessed | tf_op | source)
XLA Modules:
  0.0 44.6 jit_solution(4352442894746676422)
XLA Ops:
  0.7 42.9 %shard_map.73.result = bf16[8,8,8,768]{3,2,1,0:T(8,128)(2,1)S(1)} custom-call(s32[1]{0:T(128)S(6)} %copy.8.shift_ref, s32[32]{0:T(128)} %group_ref.1, bf16[8,8,8,768]{3,2,1,0:T(8,128)(2,1)} %bitcast.2, bf16[768,2304]{1,0:T(8,128)(2,1)} %wsq_h.1, bf16[768,768]{1,0:T(8,128)(2,1)} %wso_h.1, bf16[768,2304]{1,0:T(8,128)(2,1)} %wtq_h.1, bf16[768,768]{1,0:T(8,128)(2,1)} %wto_h.1), custom_call_target="tpu_custom_call" | custom-call | tf_op jit(solution)/shard_map/pallas_call | solution.py:449
  43.6 0.9 %shard_map.74 = bf16[8,8,8,768]{3,2,1,0:T(8,128)(2,1)} custom-call(bf16[8,8,8,768]{3,2,1,0:T(8,128)(2,1)S(1)} %shard_map.73.result), custom_call_target="tpu_custom_call" | custom-call | tf_op jit(solution)/shard_map/pallas_call | solution.py:497

commit v6 on v5

--- a/solution.py
+++ b/solution.py
@@ -435,9 +435,11 @@
 
 
 def write_out(result, out, sem):
-    copy = pltpu.make_async_copy(result, out, sem)
-    copy.start()
-    copy.wait()
+    copies = [pltpu.make_async_copy(result.at[i], out.at[i], sem.at[i]) for i in range(8)]
+    for copy in copies:
+        copy.start()
+    for copy in copies:
+        copy.wait()
 
 
 def per_device(
@@ -499,7 +501,7 @@
         out_shape=jax.ShapeDtypeStruct((8, 8, 8, D), BF16),
         in_specs=[anywhere],
         out_specs=anywhere,
-        scratch_shapes=[dma],
+        scratch_shapes=[dma((8,))],
     )(pltpu.with_memory_space_constraint(result, pltpu.VMEM))
     return written.reshape(tokens.shape)
 

time: 44.7 us -> 44.7 us (level)
  no operation moved by 1% of the time
where the time goes in v6:
time: 44.7 us
  Pallas kernels  43.8 us (98%)
  between operations  0.82 us (2%)
    pallas_call x1, Pallas kernels, per_device(): pl.pallas_call(kernel, out_shape=pltpu.VMEM((8, 8, 8, D), BF16), in_specs...  42.9 us
    pallas_call x1, Pallas kernels, per_device(): pl.pallas_call(write_out, out_shape=jax.ShapeDtypeStruct((8, 8, 8, D), BF...  0.94 us

profile of v6, /device:TPU:1, one launch (start us, length us, event | category | flops | bytes accessed | tf_op | source)
XLA Modules:
  0.0 44.7 jit_solution(1787642980643388223)
XLA Ops:
  0.7 42.9 %shard_map.73.result = bf16[8,8,8,768]{3,2,1,0:T(8,128)(2,1)S(1)} custom-call(s32[1]{0:T(128)S(6)} %copy.8.shift_ref, s32[32]{0:T(128)} %group_ref.1, bf16[8,8,8,768]{3,2,1,0:T(8,128)(2,1)} %bitcast.2, bf16[768,2304]{1,0:T(8,128)(2,1)} %wsq_h.1, bf16[768,768]{1,0:T(8,128)(2,1)} %wso_h.1, bf16[768,2304]{1,0:T(8,128)(2,1)} %wtq_h.1, bf16[768,768]{1,0:T(8,128)(2,1)} %wto_h.1), custom_call_target="tpu_custom_call" | custom-call | tf_op jit(solution)/shard_map/pallas_call | solution.py:451
  43.6 0.9 %shard_map.74 = bf16[8,8,8,768]{3,2,1,0:T(8,128)(2,1)} custom-call(bf16[8,8,8,768]{3,2,1,0:T(8,128)(2,1)S(1)} %shard_map.73.result), custom_call_target="tpu_custom_call" | custom-call | tf_op jit(solution)/shard_map/pallas_call | solution.py:499
